TPU v7x, 256 devices: a whole 4x4x8 slice. The times are simulated.
256 devices in a mesh: lat: 8 (over z_hi, y), lon: 32 (over z_lo, x, core).
Axes of the slice: x: 4, y: 4, z: 8 (z_hi: 2, z_lo: 4; z = z_hi * 4 + z_lo), core: 2. Of those that a mesh axis runs over, the one named last changes fastest.
Arguments:
- species_amounts: float32 [32, 128, 32, 128], P('lat', 'lon'), may hold values from 0.1 to 3
- thermal_anomaly: float32 [32, 128, 32], P('lat', 'lon'), may hold values from -1 to 1
- solar_flux_factor: float32 [32, 128], P('lat', 'lon'), may hold values from 0 to 1
- inner_iterations: int32 [32, 128], P('lat', 'lon'), may hold values from 4 to 36
- reference_speed: float32 [512], replicated, may hold values from 0.01 to 3
- thermal_response: float32 [512], replicated, may hold values from -1 to 1
- photo_breakup: float32 [512], replicated, may hold values from 0.03 to 3
- reaction_recipe: int32 [4, 512], replicated, may hold values from 0 to 127
- eastward_wind_ratio: float32 [32, 32, 128], P('lon', 'lat'), may hold values from -0.95 to 0.95
- northward_wind_ratio: float32 [32, 32, 128], P('lon', 'lat'), may hold values from -0.95 to 0.95
Outputs:
- transported: float32 [32, 128, 32, 128], P('lat', 'lon')
Inputs may be any that keep to these rules, and one draw needn't show every extreme that they name: `reaction_recipe`: row 0 and row 1 name the two reactants of each reaction, rows 2 and 3 its two products.
All inputs are finite; a program needn't handle non-finite values.
Results may differ from a plain program's by a relative error of at most 0.0003.
Values sent between devices are 32-bit elements; how exact they have to be, the bound alone decides.
No kernel may reach another device: no remote copies, remote signals or barrier semaphores. Data moves between devices by JAX's collectives and lax.ppermute only.
A program may use at most 64 MiB of HBM per device.

v0:
```python
import jax
import jax.numpy as jnp
from jax import lax
from jax.sharding import PartitionSpec as P

ADV_STEPS = 2


def with_halo(block, sides, width):
    for axis, dim in sides:
        count = lax.axis_size(axis)
        forward = [(i, i + 1) for i in range(count - 1)]
        backward = [(target, source) for source, target in forward]
        low = lax.ppermute(
            lax.slice_in_dim(block, block.shape[dim] - width, None, axis=dim), axis, forward
        )
        high = lax.ppermute(lax.slice_in_dim(block, 0, width, axis=dim), axis, backward)
        block = jnp.concatenate([low, block, high], axis=dim)
    return block


def slice_axis(array, start, count, along):
    return lax.slice_in_dim(array, start, start + count, axis=along)


def flux_sweep(padded, courant_pad, along, length):
    far_left = slice_axis(padded, 0, length + 3, along)
    near_left = slice_axis(padded, 1, length + 3, along)
    near_right = slice_axis(padded, 2, length + 3, along)
    far_right = slice_axis(padded, 3, length + 3, along)
    edges = 7.0 / 12.0 * (near_left + near_right) - 1.0 / 12.0 * (far_left + far_right)
    edges = jnp.minimum(
        jnp.maximum(edges, jnp.minimum(near_left, near_right)), jnp.maximum(near_left, near_right)
    )
    cell_means = slice_axis(padded, 2, length + 2, along)
    left_edge = slice_axis(edges, 0, length + 2, along)
    right_edge = slice_axis(edges, 1, length + 2, along)
    edge_jump = right_edge - left_edge
    curvature = 6.0 * cell_means - 3.0 * (left_edge + right_edge)
    courant = slice_axis(courant_pad, 3, length + 1, along)
    magnitude = jnp.abs(courant)
    from_left = slice_axis(right_edge, 0, length + 1, along) - 0.5 * courant * (
        slice_axis(edge_jump, 0, length + 1, along)
        - (1.0 - 2.0 / 3.0 * courant) * slice_axis(curvature, 0, length + 1, along)
    )
    from_right = slice_axis(left_edge, 1, length + 1, along) + 0.5 * magnitude * (
        slice_axis(edge_jump, 1, length + 1, along)
        + (1.0 - 2.0 / 3.0 * magnitude) * slice_axis(curvature, 1, length + 1, along)
    )
    face_flux = courant * jnp.where(courant >= 0.0, from_left, from_right)
    interior = slice_axis(padded, 3, length, along)
    return interior - (
        slice_axis(face_flux, 1, length, along) - slice_axis(face_flux, 0, length, along)
    )


def wrap_pad(array, along):
    extent = array.shape[along]
    return jnp.concatenate(
        [slice_axis(array, extent - 3, 3, along), array, slice_axis(array, 0, 3, along)], axis=along
    )


def reaction_tables(reaction_recipe, species):
    species_ids = lax.broadcasted_iota(jnp.int32, (reaction_recipe.shape[1], species), 1)
    picks = [
        (reaction_recipe[which_row][:, None] == species_ids).astype(jnp.float32)
        for which_row in range(4)
    ]
    making = picks[2] + picks[3]
    losing = jnp.concatenate([picks[0], picks[1]], axis=0)
    return (making, losing)


def react_block(
    species_amounts,
    thermal_anomaly,
    solar_flux_factor,
    inner_iterations,
    reference_speed,
    thermal_response,
    photo_breakup,
    reaction_recipe,
    making,
    losing,
):
    species = species_amounts.shape[-1]
    flat_rows = species_amounts.reshape(-1, species)
    local_warmth = thermal_anomaly.reshape(-1, 1)
    local_irradiance = jnp.broadcast_to(
        solar_flux_factor[:, :, None], thermal_anomaly.shape
    ).reshape(-1, 1)
    mesh_box_total = jnp.broadcast_to(inner_iterations[:, :, None], thermal_anomaly.shape).reshape(
        -1, 1
    )
    speed_coefficient = (
        reference_speed * jnp.exp(thermal_response * local_warmth)
        + photo_breakup * local_irradiance
    )
    substep = 1.0 / mesh_box_total.astype(jnp.float32)
    longest = jnp.max(inner_iterations)

    def advance(step_index, current):
        first_conc = jnp.take(current, reaction_recipe[0], axis=1)
        second_conc = jnp.take(current, reaction_recipe[1], axis=1)
        reaction_flow = speed_coefficient * first_conc * second_conc
        produced = jnp.dot(
            reaction_flow,
            making,
            precision=lax.Precision.HIGHEST,
            preferred_element_type=jnp.float32,
        )
        lost_terms = jnp.concatenate(
            [speed_coefficient * second_conc, speed_coefficient * first_conc], axis=1
        )
        lost_rate = jnp.dot(
            lost_terms, losing, precision=lax.Precision.HIGHEST, preferred_element_type=jnp.float32
        )
        updated = (current + substep * produced) / (1.0 + substep * lost_rate)
        return jnp.where(step_index < mesh_box_total, updated, current)

    result = lax.fori_loop(0, longest, advance, flat_rows)
    return result.reshape(species_amounts.shape)


def per_device(
    species_amounts,
    thermal_anomaly,
    solar_flux_factor,
    inner_iterations,
    reference_speed,
    thermal_response,
    photo_breakup,
    reaction_recipe,
    eastward_wind_ratio,
    northward_wind_ratio,
):
    making, losing = reaction_tables(reaction_recipe, species_amounts.shape[-1])
    constants = (reference_speed, thermal_response, photo_breakup, reaction_recipe, making, losing)
    midway_stack_total = species_amounts.shape[1] // 2
    reacted_first = react_block(
        species_amounts[:, :midway_stack_total],
        thermal_anomaly[:, :midway_stack_total],
        solar_flux_factor[:, :midway_stack_total],
        inner_iterations[:, :midway_stack_total],
        *constants
    )
    reacted_local = react_block(
        species_amounts[:, midway_stack_total:],
        thermal_anomaly[:, midway_stack_total:],
        solar_flux_factor[:, midway_stack_total:],
        inner_iterations[:, midway_stack_total:],
        *constants
    )
    settled_columns = jnp.concatenate([reacted_first, reacted_local], axis=1)
    lat_rows = species_amounts.shape[0]
    row_ids = lax.axis_index("lat") * lat_rows + lax.broadcasted_iota(
        jnp.int32, (lat_rows, 1, 1, 1), 0
    )
    carried_quantity = lax.all_to_all(
        settled_columns, "lon", split_axis=2, concat_axis=1, tiled=True
    )
    east_faces = jnp.transpose(eastward_wind_ratio, (1, 2, 0))[..., None]
    south_faces = jnp.where(
        row_ids > 0, jnp.transpose(northward_wind_ratio, (1, 2, 0))[..., None], 0.0
    )
    east_pad = wrap_pad(east_faces, 1)
    for sweep_index in range(ADV_STEPS):
        carried_quantity = flux_sweep(
            wrap_pad(carried_quantity, 1), east_pad, 1, carried_quantity.shape[1]
        )
        rimmed, south_pad = (
            with_halo(carried_quantity, (("lat", 0),), 3),
            with_halo(south_faces, (("lat", 0),), 3),
        )
        carried_quantity = flux_sweep(rimmed, south_pad, 0, lat_rows)
    return lax.all_to_all(carried_quantity, "lon", split_axis=1, concat_axis=2, tiled=True)


def solution(mesh):
    return jax.shard_map(
        per_device,
        mesh=mesh,
        in_specs=(
            P("lat", "lon", None, None),
            P("lat", "lon", None),
            P("lat", "lon"),
            P("lat", "lon"),
            P(),
            P(),
            P(),
            P(),
            P("lon", "lat", None),
            P("lon", "lat", None),
        ),
        out_specs=P("lat", "lon", None, None),
        check_vma=False,
    )
```

profile of v0, /device:TPU:192, one launch (start us, length us, event | category | flops | bytes accessed | tf_op | source)
XLA Modules:
  0.0 634.3 jit_solution(11603967934945365534)
XLA Ops:
  4.6 245.7 %while.24 = (s32[]{:T(128)}, f32[256,128]{1,0:T(8,128)S(1)}, s32[]{:T(128)}, s32[4,512]{1,0:T(4,128)S(1)}, f32[1024,128]{1,0:T(8,128)S(1)}, /*index=5*/s32[4,2]{...) while((s32[]{:T(128)}, f32[256,128]{1,0:T(8,128)S(1)}, ...), condition=%wide.region_2.4_spmd.clone.clone, body=%wide.region_1.3_spmd.clone.clone.sunk | while | flops 606088960 | bytes 7662761 | solution.py:122
  9.2 1.8 fusion.135
  16.8 1.8 fusion.135
  24.5 1.8 fusion.135
  32.1 1.8 fusion.135
  39.8 1.8 fusion.135
  47.4 1.8 fusion.135
  55.1 1.8 fusion.135
  62.8 1.8 fusion.135
  78.1 1.8 fusion.135
  85.7 1.8 fusion.135
  93.4 1.8 fusion.135
  101.1 1.8 fusion.135
  108.7 1.8 fusion.135
  116.4 1.8 fusion.135
  131.7 1.8 fusion.135
  147.0 1.8 fusion.135
  154.7 1.8 fusion.135
  162.3 1.8 fusion.135
  170.0 1.8 fusion.135
  177.6 1.8 fusion.135
  185.3 1.8 fusion.135
  200.6 1.8 fusion.135
  215.9 1.8 fusion.135
  223.6 1.8 fusion.135
  231.3 1.8 fusion.135
  238.9 1.8 fusion.135
  250.5 263.1 %while.25 = (s32[]{:T(128)}, f32[256,128]{1,0:T(8,128)S(1)}, s32[]{:T(128)}, s32[4,512]{1,0:T(4,128)S(1)}, f32[1024,128]{1,0:T(8,128)S(1)}, /*index=5*/s32[4,2]{...) while((s32[]{:T(128)}, f32[256,128]{1,0:T(8,128)S(1)}, ...), condition=%wide.region_5.7_spmd.clone.clone, body=%wide.region_4.6_spmd.clone.clone.sunk | while | flops 606088960 | bytes 7662761 | solution.py:122
  255.2 1.8 fusion.141
  270.6 1.8 fusion.141
  278.3 1.8 fusion.141
  286.0 1.8 fusion.141
  301.5 1.8 fusion.141
  309.2 1.8 fusion.141
  324.6 1.8 fusion.141
  332.3 1.8 fusion.141
  340.0 1.8 fusion.141
  347.8 1.8 fusion.141
  355.5 1.8 fusion.141
  370.9 1.8 fusion.141
  378.6 1.8 fusion.141
  394.1 1.8 fusion.141
  401.8 1.8 fusion.141
  409.5 1.8 fusion.141
  417.2 1.8 fusion.141
  424.9 1.8 fusion.141
  440.4 1.8 fusion.141
  448.1 1.8 fusion.141
  463.5 1.8 fusion.141
  471.2 1.8 fusion.141
  486.7 1.8 fusion.141
  494.4 1.8 fusion.141
  502.1 1.8 fusion.141
  509.8 1.8 fusion.141
  514.5 53.3 %all-to-all-start = ((f32[4,4,32,128]{3,1,0,2:T(4,128)}), f32[4,4,32,128]{3,1,0,2:T(4,128)S(1)}, u32[]{:S(2)}, u32[]{:S(2)}) async-start(f32[4,4,32,128]{3,1,0,2:T(4,128)} %copy.49), calls=%async_computation | async-start | bytes 524288 | tf_op jit(solution)/shard_map/all_to_all | solution.py:160
  568.6 4.3 collective-permute-start
  574.2 3.0 all-to-all-done
  578.2 2.2 collective-permute-start.1
  580.4 9.8 %collective-permute-start.2 = (f32[3,128,1,128]{3,1,0,2:T(8,128)S(1)}, f32[3,128,1,128]{3,1,0,2:T(8,128)S(1)}, u32[]{:S(2)}, u32[]{:S(2)}) collective-permute-start(f32[3,128,1,128]{3,1,0,2:T(8,128)S(1)} %get-tuple-element.337), channel_id=1, source_target_pairs={{32,0},{64,32},{96,64},{128,96},{160,128},{192,160},{224,192},{33,... | collective-permute-start | bytes 589832 | tf_op jit(solution)/shard_map/ppermute | solution.py:17
  590.2 6.9 %collective-permute-done.1 = f32[3,128,1,128]{3,1,0,2:T(8,128)S(1)} collective-permute-done((f32[3,128,1,128]{3,1,0,2:T(8,128)S(1)}, f32[3,128,1,128]{3,1,0,2:T(8,128)S(1)}, u32[]{:S(2)}, u32[]{:S(2)}) %collective-permute-start.1) | collective-permute-done | bytes 196640 | tf_op jit(solution)/shard_map/ppermute | solution.py:14
  600.2 1.9 collective-permute-start.3
  602.2 10.4 %collective-permute-start.4 = (f32[3,128,1,128]{3,1,0,2:T(8,128)S(1)}, f32[3,128,1,128]{3,1,0,2:T(8,128)S(1)}, u32[]{:S(2)}, u32[]{:S(2)}) collective-permute-start(f32[3,128,1,128]{3,1,0,2:T(8,128)S(1)} %get-tuple-element.333), channel_id=1, source_target_pairs={{32,0},{64,32},{96,64},{128,96},{160,128},{192,160},{224,192},{33,... | collective-permute-start | bytes 589832 | tf_op jit(solution)/shard_map/ppermute | solution.py:17
  612.6 4.0 collective-permute-done.3
  618.8 14.7 %all_to_all.36 = f32[4,128,1,128]{3,0,2,1:T(4,128)S(1)} all-to-all(f32[4,128,1,128]{3,0,2,1:T(4,128)S(1)} %copy.51), channel_id=1, replica_groups=mesh['lat'=8,'lon'=32] {'lon'}, dimensions={1} | all-to-all | bytes 524288 | tf_op jit(solution)/shard_map/all_to_all | solution.py:177
  (1075 shorter events, 377.2 us)
Async XLA Ops:
  0.0 0.9 copy-start.6
  1.7 1.0 copy-start.5
  2.7 0.7 copy-start.7
  3.8 0.7 copy-start.2
  3.8 0.7 copy-start.3
  3.9 0.7 copy-start
  3.9 0.7 copy-start.1
  514.5 62.7 %all-to-all-start = ((f32[4,4,32,128]{3,1,0,2:T(4,128)}), f32[4,4,32,128]{3,1,0,2:T(4,128)S(1)}, u32[]{:S(2)}, u32[]{:S(2)}) async-start(f32[4,4,32,128]{3,1,0,2:T(4,128)} %copy.49), calls=%async_computation | async-start | bytes 524288 | tf_op jit(solution)/shard_map/all_to_all | solution.py:160
  567.9 0.7 copy-start.8
  568.6 4.3 copy-start.4
  568.6 5.6 collective-permute-start
  578.2 19.0 %collective-permute-start.1 = (f32[3,128,1,128]{3,1,0,2:T(8,128)S(1)}, f32[3,128,1,128]{3,1,0,2:T(8,128)S(1)}, u32[]{:S(2)}, u32[]{:S(2)}) collective-permute-start(f32[3,128,1,128]{3,1,0,2:T(8,128)S(1)} %get-tuple-element.336), channel_id=1, source_target_pairs={{0,32},{32,64},{64,96},{96,128},{128,160},{160,192},{192,224},{1,3... | collective-permute-start | bytes 589832 | tf_op jit(solution)/shard_map/ppermute | solution.py:14
  580.4 18.0 %collective-permute-start.2 = (f32[3,128,1,128]{3,1,0,2:T(8,128)S(1)}, f32[3,128,1,128]{3,1,0,2:T(8,128)S(1)}, u32[]{:S(2)}, u32[]{:S(2)}) collective-permute-start(f32[3,128,1,128]{3,1,0,2:T(8,128)S(1)} %get-tuple-element.337), channel_id=1, source_target_pairs={{32,0},{64,32},{96,64},{128,96},{160,128},{192,160},{224,192},{33,... | collective-permute-start | bytes 589832 | tf_op jit(solution)/shard_map/ppermute | solution.py:17
  600.2 16.3 %collective-permute-start.3 = (f32[3,128,1,128]{3,1,0,2:T(8,128)S(1)}, f32[3,128,1,128]{3,1,0,2:T(8,128)S(1)}, u32[]{:S(2)}, u32[]{:S(2)}) collective-permute-start(f32[3,128,1,128]{3,1,0,2:T(8,128)S(1)} %get-tuple-element.332), channel_id=1, source_target_pairs={{0,32},{32,64},{64,96},{96,128},{128,160},{160,192},{192,224},{1,3... | collective-permute-start | bytes 589832 | tf_op jit(solution)/shard_map/ppermute | solution.py:14
  602.2 15.5 %collective-permute-start.4 = (f32[3,128,1,128]{3,1,0,2:T(8,128)S(1)}, f32[3,128,1,128]{3,1,0,2:T(8,128)S(1)}, u32[]{:S(2)}, u32[]{:S(2)}) collective-permute-start(f32[3,128,1,128]{3,1,0,2:T(8,128)S(1)} %get-tuple-element.333), channel_id=1, source_target_pairs={{32,0},{64,32},{96,64},{128,96},{160,128},{192,160},{224,192},{33,... | collective-permute-start | bytes 589832 | tf_op jit(solution)/shard_map/ppermute | solution.py:17
where the time goes:
time: 647 us; the launch traced here: 634 us
  local copies, waits for them, and re-layouts  231 us (36%)
  matrix products  201 us (31%)
  starting transfers between devices  82 us (13%)
  loops' own time  51.9 us (8%)
  other arithmetic  35.7 us (6%)
  waiting for transfers between devices  17.4 us (3%)
  blocking collectives  14.7 us (2%)
    dot_general x66, matrix products, advance(): jnp.dot(lost_terms, losing, precision=lax.Precision.HIGHEST, preferred_el...  120 us
    gather x66, local copies, waits for them, and re-layouts, advance(): second_conc = jnp.take(current, reaction_recipe[1], axis=1)  104 us
    gather x66, local copies, waits for them, and re-layouts, advance(): first_conc = jnp.take(current, reaction_recipe[0], axis=1)  104 us
    dot_general x66, matrix products, advance(): jnp.dot(reaction_flow, making, precision=lax.Precision.HIGHEST, preferred...  81.9 us
    all_to_all x1, starting transfers between devices, per_device(): lax.all_to_all(settled_columns, 'lon', split_axis=2, concat_axis=1, tiled...  53.3 us
    another operation x2, loops' own time, react_block(): result = lax.fori_loop(0, longest, advance, flat_rows)  51.9 us
    mul x66, other arithmetic, advance(): speed_coefficient * second_conc  27 us
    ppermute x3, starting transfers between devices, with_halo(): lax.ppermute(lax.slice_in_dim(block, 0, width, axis=dim), axis, backward)  24.6 us
  transfers between devices with their start and end apart: 6, of which 6 were waited for; matrix products, arithmetic and copies ran while one was open for 0% of the time, Pallas kernels for 0%

commit v1 on v0

v1 whole, which is shorter than its diff:
```python
import functools

import jax
import jax.numpy as jnp
from jax import lax
from jax.experimental import pallas as pl
from jax.experimental.pallas import tpu as pltpu
from jax.sharding import PartitionSpec as P

ADV_STEPS = 2
LANES = 16
FLOOR = 1e-30
GROUP = 8
UNROLL = 2
SHUFFLED = 1
PARTS = 2
INPUTS = 8
BF = jnp.bfloat16
F32 = jnp.float32
VMEM = pl.BlockSpec(memory_space=pltpu.VMEM)
SMEM = pl.BlockSpec(memory_space=pltpu.SMEM)


def store_parts(refs, at, value):
    size = value.shape[0] // len(refs)
    for part, ref in enumerate(refs):
        ref[at] = value[part * size : (part + 1) * size]


def load_parts(refs, at):
    return jnp.concatenate([ref[at] for ref in refs], axis=0)


def one_hot(row, size):
    ids = lax.broadcasted_iota(jnp.int32, (size, row.shape[1]), 0)
    return (jnp.broadcast_to(row, ids.shape) == ids).astype(F32)


def split_halves(value):
    high = value.astype(BF)
    return high, (value - high.astype(F32)).astype(BF)


def pack_winds(eastward, northward, rows, turned, packed):
    n_lat, n_lon = eastward.shape[1:]
    owners = packed.shape[0]
    own = n_lon // owners
    rows[...] = jnp.zeros_like(rows)
    rows[:n_lat, :] = eastward[0]
    first = lax.broadcasted_iota(jnp.int32, (n_lat, n_lon), 0) + lax.axis_index("lat") == 0
    rows[n_lat : 2 * n_lat, :] = jnp.where(first, 0.0, northward[0])
    turned[...] = rows[...].T
    pieces = [turned[pl.ds(i, owners, stride=own), :] for i in range(own)]
    pieces.append(jnp.concatenate([pieces[0][1:], pieces[0][:1]], axis=0))
    total = pieces[0]
    for i in range(1, own + 1):
        total = total + pltpu.roll(pieces[i], LANES * i, axis=1)
    packed[:, 0, :] = total


def chemistry_kernel(
    counts, solar, *refs, group
):
    sources, outputs = refs[:INPUTS], refs[INPUTS : INPUTS + 2 + 2 * PARTS]
    settled, packed = outputs[:2]
    to_east, to_west = outputs[2 : 2 + PARTS], outputs[2 + PARTS :]
    refs = refs[INPUTS + 2 + 2 * PARTS :]
    held, (order, rates, state, sums, gather, square, turned, waiting, arrived) = (
        refs[:INPUTS], refs[INPUTS:]
    )
    copies = [
        pltpu.make_async_copy(source, target, arrived.at[i])
        for i, (source, target) in enumerate(zip(sources, held))
    ]
    for copy in copies:
        copy.start()
    recipe, eastward, northward, speed, response, photo, warmth, species = held
    n_lat, n_lon, levels, kinds = species.shape
    reactions = recipe.shape[1]
    columns = n_lat * n_lon
    chunks = reactions // 128

    flat = [counts[i // n_lon, i % n_lon] for i in range(columns)]
    for i in range(columns):
        rank = jnp.int32(0)
        for j in range(columns):
            if j != i:
                ahead = flat[j] >= flat[i] if j < i else flat[j] > flat[i]
                rank = rank + ahead.astype(jnp.int32)
        order[rank] = i

    def place(slot):
        column = order[slot]
        return column // n_lon, lax.rem(column, n_lon)

    def count_of(slot):
        a, b = place(slot)
        return counts[a, b]

    for copy in copies:
        copy.wait()
    pack_winds(eastward, northward, square, turned, packed)

    for chunk in range(chunks):
        lanes = slice(chunk * 128, (chunk + 1) * 128)
        first, second, third, fourth = [one_hot(recipe[r : r + 1, lanes], kinds) for r in range(4)]
        both = jnp.concatenate([first, second], axis=1).astype(BF)
        gather[chunk, :kinds, :] = both
        gather[chunk, kinds:, :] = both
        ends = jnp.concatenate([(third + fourth).T, (first + second).T], axis=1).astype(BF)
        sums[chunk * 256 : chunk * 256 + 128, :] = ends
        sums[chunk * 256 + 128 : chunk * 256 + 256, :] = ends

    for i in range(columns):
        a, b = place(i)
        square[i : i + 1, :levels] = warmth[a, pl.ds(b, 1), :]
    warm_columns = square[...].T
    exponent, base, light = response[...], speed[...], photo[...]
    for i in range(columns):
        a, b = place(i)
        rows = slice(i * levels, (i + 1) * levels)
        warm = jnp.broadcast_to(warm_columns[:levels, i : i + 1], (levels, reactions))
        rates[rows, :] = base * jnp.exp(exponent * warm) + light * solar[a, b]
        state[rows, :] = jnp.maximum(species[a, b], FLOOR)

    def sums_of(start, length):
        rows = slice(start * levels, (start + length) * levels)
        amounts = state[rows, :]
        picked = jnp.concatenate(split_halves(amounts), axis=1)
        flows = []
        for chunk in range(chunks):
            lanes = slice(chunk * 128, (chunk + 1) * 128)
            if chunk < chunks - SHUFFLED:
                pair = jnp.dot(picked, gather[chunk], preferred_element_type=F32)
                first, second = pair[:, :128], pair[:, 128:]
            else:
                first, second = [
                    jnp.take_along_axis(
                        amounts,
                        jnp.broadcast_to(recipe[r : r + 1, lanes], amounts.shape),
                        axis=1,
                        mode="promise_in_bounds",
                    )
                    for r in range(2)
                ]
            flows.extend(split_halves(rates[rows, lanes] * first * second))
        return jnp.dot(jnp.concatenate(flows, axis=1), sums[...], preferred_element_type=F32)

    def update(start, length, both, t, ns, steps):
        for i in range(length):
            rows = slice((start + i) * levels, (start + i + 1) * levels)
            part = slice(i * levels, (i + 1) * levels)
            amount, n, step = state[rows, :], ns[start + i], steps[start + i]
            grown = amount + step * both[part, :kinds]
            kept = amount / (amount + step * both[part, kinds:])
            state[rows, :] = jnp.where(t < n, jnp.maximum(grown * kept, FLOOR), amount)

    def run(live, begin, trips):
        half = live // 2
        ns = [count_of(i) for i in range(live)]
        steps = [1.0 / n.astype(F32) for n in ns]
        rows = slice(0, half * levels)

        @pl.when(trips > 0)
        def _():
            waiting[rows, :] = sums_of(half, half)

            def substeps(trip, carry):
                held = waiting[rows, :]
                for offset in range(UNROLL):
                    t = begin + trip * UNROLL + offset
                    both = sums_of(0, half)
                    update(half, half, held, t, ns, steps)
                    held = sums_of(half, half)
                    update(0, half, both, t, ns, steps)
                waiting[rows, :] = held
                return carry

            lax.fori_loop(0, trips, substeps, 0)

    begin = jnp.int32(0)
    for live in range(columns, 0, -group):
        trips = jnp.maximum(count_of(live - group) - begin + UNROLL - 1, 0) // UNROLL
        run(live, begin, trips)
        begin = begin + trips * UNROLL

    for i in range(columns):
        a, b = place(i)
        value = state[i * levels : (i + 1) * levels, :]
        settled[a, b] = value

        @pl.when(b > 0)
        def _():
            store_parts(to_east, (a, jnp.maximum(b - 1, 0)), value)

        @pl.when(b < n_lon - 1)
        def _():
            store_parts(to_west, (a, jnp.minimum(b, n_lon - 2)), value)


def chemistry(counts, solar, *arrays):
    recipe, eastward, species = arrays[0], arrays[1], arrays[-1]
    n_lat, n_lon, levels, kinds = species.shape
    reactions, longitudes = recipe.shape[1], eastward.shape[2]
    columns = n_lat * n_lon
    halo = jax.ShapeDtypeStruct((n_lat, n_lon - 1, levels // PARTS, kinds), F32)
    return pl.pallas_call(
        functools.partial(chemistry_kernel, group=GROUP),
        out_shape=(
            jax.ShapeDtypeStruct(species.shape, F32),
            jax.ShapeDtypeStruct((longitudes // n_lon, 1, 128), F32),
        )
        + (halo,) * (2 * PARTS),
        in_specs=[SMEM, SMEM] + [pl.BlockSpec(memory_space=pltpu.HBM)] * INPUTS,
        out_specs=(VMEM,) * (2 + 2 * PARTS),
        scratch_shapes=[pltpu.VMEM(array.shape, array.dtype) for array in arrays]
        + [
            pltpu.SMEM((columns,), jnp.int32),
            pltpu.VMEM((columns * levels, reactions), F32),
            pltpu.VMEM((columns * levels, kinds), F32),
            pltpu.VMEM((2 * reactions, 2 * kinds), BF),
            pltpu.VMEM((reactions // 128, 2 * kinds, 256), BF),
            pltpu.VMEM((128, 128), F32),
            pltpu.VMEM((128, 128), F32),
            pltpu.VMEM((columns * levels // 2, 2 * kinds), F32),
            pltpu.SemaphoreType.DMA((INPUTS,)),
        ],
        compiler_params=pltpu.CompilerParams(vmem_limit_bytes=62 << 20),
        cost_estimate=pl.CostEstimate(
            flops=int(2e10), bytes_accessed=2 << 20, transcendentals=0
        ),
        name="chemistry",
    )(counts, solar, *arrays)


def sweep_line(cells, faces):
    count = len(cells) - 6
    edges = {}
    for k in range(2, count + 5):
        far_left, left, right, far_right = cells[k - 2 : k + 2]
        edge = (7.0 / 12.0) * (left + right) - (1.0 / 12.0) * (far_left + far_right)
        edges[k] = jnp.minimum(
            jnp.maximum(edge, jnp.minimum(left, right)), jnp.maximum(left, right)
        )
    jumps, curves = {}, {}
    for k in range(2, count + 4):
        jumps[k] = edges[k + 1] - edges[k]
        curves[k] = 6.0 * cells[k] - 3.0 * (edges[k] + edges[k + 1])
    flux = []
    for k in range(count + 1):
        courant, at = faces[k], k + 3
        size = jnp.abs(courant)
        upwind = courant >= 0.0
        jump = jnp.where(upwind, -jumps[at - 1], jumps[at])
        curve = jnp.where(upwind, curves[at - 1], curves[at])
        value = edges[at] + 0.5 * size * (jump + (1.0 - (2.0 / 3.0) * size) * curve)
        flux.append(courant * value)
    return [cells[k + 3] - (flux[k + 1] - flux[k]) for k in range(count)]


def spread(wind, lane, tile):
    return jnp.broadcast_to(wind[:, lane : lane + 1], tile)


def wind_rows(wind, rows):
    for i in range(rows.shape[0]):
        rows[i : i + 1, :] = wind[i]
    return rows[...]


def zonal_kernel(block, wind, *refs):
    low, high = refs[:PARTS], refs[PARTS : 2 * PARTS]
    swept, inner, outer, rows = refs[2 * PARTS :]
    n_lat, n_lon = block.shape[:2]
    tile = block.shape[2:]
    winds = wind_rows(wind, rows)
    even = lax.rem(lax.axis_index("lat"), 2) == 0
    inner[(n_lat - 1) * n_lon] = winds
    outer[(n_lat - 1) * n_lon] = winds
    lines = []
    for a in range(n_lat):
        cells = [load_parts(low, (a, i)) for i in range(3)]
        cells += [block[a, i] for i in range(n_lon)]
        cells += [load_parts(high, (a, i)) for i in range(3)]
        faces = [spread(winds, LANES * k + a, tile) for k in range(n_lon + 1)]
        lines.append(sweep_line(cells, faces))
        for i, value in enumerate(lines[a]):
            swept[a, i] = value
            if a > 0:
                at, below = (a - 1) * n_lon + i, lines[a - 1][i]
                inner[at] = jnp.where(even, value, below)
                outer[at] = jnp.where(even, below, value)


def meridional_kernel(block, wind, inner, outer, swept, *refs):
    *sends, rows = refs
    n_lat, n_lon = block.shape[:2]
    tile = block.shape[2:]
    band = lax.axis_index("lat")
    even = lax.rem(band, 2) == 0
    south_end, north_end = band == 0, band == lax.axis_size("lat") - 1

    def low(at):
        return jnp.where(south_end, 0.0, jnp.where(even, outer[at], inner[at]))

    def high(at):
        return jnp.where(north_end, 0.0, jnp.where(even, inner[at], outer[at]))

    winds, above = wind_rows(wind, rows), high(3 * n_lon)
    for i in range(n_lon):
        cells = [low(a * n_lon + i) for a in range(3)]
        cells += [block[a, i] for a in range(n_lat)]
        cells += [high(a * n_lon + i) for a in range(3)]
        faces = [spread(winds, LANES * i + n_lat + k, tile) for k in range(n_lat)]
        faces.append(spread(above, LANES * i + n_lat, tile))
        for a, value in enumerate(sweep_line(cells, faces)):
            swept[a, i] = value
            if sends and i > 0:
                store_parts(sends[:PARTS], (a, i - 1), value)
            if sends and i < n_lon - 1:
                store_parts(sends[PARTS:], (a, i), value)


def sweep(kernel, block, wind, halos, sent_shapes, name):
    shapes = (block.shape,) + sent_shapes
    return pl.pallas_call(
        kernel,
        out_shape=tuple(jax.ShapeDtypeStruct(shape, F32) for shape in shapes),
        in_specs=[VMEM] * (2 + len(halos)),
        out_specs=(VMEM,) * len(shapes),
        scratch_shapes=[pltpu.VMEM((wind.shape[0], wind.shape[2]), F32)],
        compiler_params=pltpu.CompilerParams(vmem_limit_bytes=24 << 20),
        name=name,
    )(block, wind, *halos)


def per_device(
    species_amounts,
    thermal_anomaly,
    solar_flux_factor,
    inner_iterations,
    reference_speed,
    thermal_response,
    photo_breakup,
    reaction_recipe,
    eastward_wind_ratio,
    northward_wind_ratio,
):
    n_lat, n_lon, levels, kinds = species_amounts.shape
    lon_count, lat_count = lax.axis_size("lon"), lax.axis_size("lat")
    eastbound = [(i, (i + 1) % lon_count) for i in range(lon_count)]
    westbound = [(target, source) for source, target in eastbound]
    inner_pairs = [(i, i ^ 1) for i in range(lat_count)]
    outer_pairs = [(i, min(max(((i + 1) ^ 1) - 1, 0), lat_count - 1)) for i in range(lat_count)]

    block, packed, *sends = chemistry(
        inner_iterations,
        solar_flux_factor,
        reaction_recipe,
        eastward_wind_ratio,
        northward_wind_ratio,
        reference_speed[None],
        thermal_response[None],
        photo_breakup[None],
        thermal_anomaly,
        species_amounts,
    )
    wind = lax.all_to_all(packed, "lon", split_axis=0, concat_axis=0, tiled=True)
    zonal_halo = (n_lat, n_lon - 1, levels // PARTS, kinds)
    meridional_halo = ((n_lat - 1) * n_lon + 1, levels, kinds)
    for step in range(ADV_STEPS):
        halos = [
            lax.ppermute(sent, "lon", eastbound if i < PARTS else westbound)
            for i, sent in enumerate(sends)
        ]
        block, inner, outer = sweep(
            zonal_kernel, block, wind, halos, (meridional_halo,) * 2, "zonal"
        )
        outer = lax.ppermute(outer, "lat", outer_pairs)
        inner = lax.ppermute(inner, "lat", inner_pairs)
        last = step == ADV_STEPS - 1
        sent_shapes = () if last else (zonal_halo,) * (2 * PARTS)
        block, *sends = sweep(
            meridional_kernel, block, wind, (inner, outer), sent_shapes, "meridional"
        )
    return block


def solution(mesh):
    return jax.shard_map(
        per_device,
        mesh=mesh,
        in_specs=(
            P("lat", "lon", None, None),
            P("lat", "lon", None),
            P("lat", "lon"),
            P("lat", "lon"),
            P(),
            P(),
            P(),
            P(),
            P("lon", "lat", None),
            P("lon", "lat", None),
        ),
        out_specs=P("lat", "lon", None, None),
        check_vma=False,
    )
```

time: 647 us -> 91.1 us (0.14); the launches traced: 634 us -> 91.2 us
  local copies, waits for them, and re-layouts: 231 us -> 0.95 us
  matrix products: 201 us -> 0 us
  starting transfers between devices: 82 us -> 15.9 us
  loops' own time: 51.9 us -> 0 us
  other arithmetic: 35.7 us -> 0 us
  blocking collectives: 14.7 us -> 31 us
  waiting for transfers between devices: 17.4 us -> 33 us
  Pallas kernels: 0 us -> 10.3 us
    gather x132 -> x0, local copies, waits for them, and re-layouts: 208 us -> none  [the longest x66 104 us: advance(): second_conc = jnp.take(current, reaction_recipe[1], axis=1)]
    dot_general x132 -> x0, matrix products: 201 us -> none  [the longest x66 120 us: advance(): jnp.dot(lost_terms, losing, precision=lax.Precision.HIGHEST, preferred_el...]
    all_to_all x1 -> x0, starting transfers between devices: 53.3 us -> none  [per_device(): lax.all_to_all(settled_columns, 'lon', split_axis=2, concat_axis=1, tiled...]
    another operation x2 -> x0, loops' own time: 51.9 us -> none  [react_block(): result = lax.fori_loop(0, longest, advance, flat_rows)]
    mul x72 -> x0, other arithmetic: 29.4 us -> none  [the longest x66 27 us: advance(): speed_coefficient * second_conc]
    ppermute x5 -> x12, waiting for transfers between devices: 14.4 us -> 33 us  [the longest x2 22 us: per_device(): outer = lax.ppermute(outer, 'lat', outer_pairs)]
    all_to_all x1, blocking collectives: 14.7 us -> 31 us  [per_device(): lax.all_to_all(packed, 'lon', split_axis=0, concat_axis=0, tiled=True)]
    ppermute x5 -> x12, starting transfers between devices: 28.7 us -> 15.9 us  [the longest x8 8.87 us: per_device(): lax.ppermute(sent, 'lon', eastbound if i < PARTS else westbound)]
  transfers between devices with their start and end apart: 6 -> 12, of which waited for: 6 -> 7; matrix products, arithmetic and copies ran while one was open for 0% -> 0% of each run, Pallas kernels for 0% -> 0%
where the time goes in v1:
time: 91.1 us; the launch traced here: 91.2 us
  waiting for transfers between devices  33 us (36%)
  blocking collectives  31 us (34%)
  starting transfers between devices  15.9 us (17%)
  Pallas kernels  10.3 us (11%)
  local copies, waits for them, and re-layouts  0.95 us (1%)
    all_to_all x1, blocking collectives, per_device(): lax.all_to_all(packed, 'lon', split_axis=0, concat_axis=0, tiled=True)  31 us
    ppermute x2, waiting for transfers between devices, per_device(): outer = lax.ppermute(outer, 'lat', outer_pairs)  22 us
    ppermute x8, starting transfers between devices, per_device(): lax.ppermute(sent, 'lon', eastbound if i < PARTS else westbound)  8.87 us
    pallas_call x1, Pallas kernels, chemistry(): pl.pallas_call(functools.partial(chemistry_kernel, group=GROUP), out_shap...  7.99 us
    ppermute x2, waiting for transfers between devices, per_device(): inner = lax.ppermute(inner, 'lat', inner_pairs)  6 us
    ppermute x2, starting transfers between devices, per_device(): outer = lax.ppermute(outer, 'lat', outer_pairs)  5.93 us
    ppermute x8, waiting for transfers between devices, per_device(): lax.ppermute(sent, 'lon', eastbound if i < PARTS else westbound)  5.06 us
    pallas_call x4, Pallas kernels, sweep(): pl.pallas_call(kernel, out_shape=tuple((jax.ShapeDtypeStruct(shape, F32)...  2.27 us
  transfers between devices with their start and end apart: 12, of which 7 were waited for; matrix products, arithmetic and copies ran while one was open for 0% of the time, Pallas kernels for 0%

profile of v1, /device:TPU:192, one launch (start us, length us, event | category | flops | bytes accessed | tf_op | source)
XLA Modules:
  0.0 91.2 jit_solution(2856030884486690017)
XLA Ops:
  0.0 8.0 %chemistry.1 = (f32[4,4,32,128]{3,2,1,0:T(8,128)}, f32[32,1,128]{2,1,0:T(1,128)}, f32[4,3,16,128]{3,2,1,0:T(8,128)}, f32[4,3,16,128]{3,2,1,0:T(8,128)}, f32[4,3,...) custom-call(s32[4,4]{1,0:T(4,128)} %counts.1, f32[4,4]{1,0:T(4,128)} %solar.1, s32[4,512]{1,0:T(4,128)} %refs_0_.1, ...), custom_call_target="tpu_custom_call" | custom-call | flops 20000000000 | bytes 2097152 | tf_op jit(solution)/shard_map/chemistry/pallas_call | solution.py:207
  8.0 0.1 collective-permute-start
  8.1 1.6 %collective-permute-start.1 = (f32[4,3,16,128]{3,2,1,0:T(8,128)}, f32[4,3,16,128]{3,2,1,0:T(8,128)S(1)}, u32[]{:S(2)}, u32[]{:S(2)}) collective-permute-start(f32[4,3,16,128]{3,2,1,0:T(8,128)} %get-tuple-element.25), channel_id=1, source_target_pairs={{0,1},{1,2},{2,3},{3,4},{4,5},{5,6},{6,7},{7,8},{8,9},{9,10},{10,1... | collective-permute-start | bytes 294920 | tf_op jit(solution)/shard_map/ppermute | solution.py:373
  9.7 2.3 %collective-permute-start.2 = (f32[4,3,16,128]{3,2,1,0:T(8,128)}, f32[4,3,16,128]{3,2,1,0:T(8,128)S(1)}, u32[]{:S(2)}, u32[]{:S(2)}) collective-permute-start(f32[4,3,16,128]{3,2,1,0:T(8,128)} %get-tuple-element.26), channel_id=1, source_target_pairs={{1,0},{2,1},{3,2},{4,3},{5,4},{6,5},{7,6},{8,7},{9,8},{10,9},{11,1... | collective-permute-start | bytes 294920 | tf_op jit(solution)/shard_map/ppermute | solution.py:373
  12.0 0.4 collective-permute-start.3
  12.4 31.0 %all_to_all.5.wind = f32[32,1,128]{2,1,0:T(1,128)S(1)} all-to-all(f32[32,1,128]{2,1,0:T(1,128)} %get-tuple-element.23), channel_id=1, replica_groups=mesh['lat'=8,'lon'=32] {'lon'}, dimensions={0} | all-to-all | bytes 32768 | tf_op jit(solution)/shard_map/all_to_all | solution.py:368
  43.4 0.0 collective-permute-done.refs_0_
  43.4 0.0 collective-permute-done.1.refs_1_
  43.4 0.0 collective-permute-done.2.refs_2_
  43.4 0.0 collective-permute-done.3.refs_3_
  43.4 0.0 copy-start
  43.4 0.9 %copy-done = f32[4,4,32,128]{3,2,1,0:T(8,128)S(1)} copy-done((f32[4,4,32,128]{3,2,1,0:T(8,128)S(1)}, f32[4,4,32,128]{3,2,1,0:T(8,128)}, u32[]{:S(2)}) %copy-start) | copy-done | bytes 262168
  44.4 0.4 zonal.2
  44.8 1.0 %collective-permute-start.4 = (f32[13,32,128]{2,1,0:T(8,128)S(1)}, f32[13,32,128]{2,1,0:T(8,128)S(1)}, u32[]{:S(2)}, u32[]{:S(2)}) collective-permute-start(f32[13,32,128]{2,1,0:T(8,128)S(1)} %get-tuple-element.29), channel_id=1, source_target_pairs={{0,32},{32,0},{64,96},{96,64},{128,160},{160,128},{192,224},{224,1... | collective-permute-start | bytes 638984 | tf_op jit(solution)/shard_map/ppermute | solution.py:380
  45.8 4.0 %collective-permute-start.5 = (f32[13,32,128]{2,1,0:T(8,128)S(1)}, f32[13,32,128]{2,1,0:T(8,128)S(1)}, u32[]{:S(2)}, u32[]{:S(2)}) collective-permute-start(f32[13,32,128]{2,1,0:T(8,128)S(1)} %get-tuple-element.30), channel_id=1, source_target_pairs={{0,0},{32,64},{64,32},{96,128},{128,96},{160,192},{192,160},{224,2... | collective-permute-start | bytes 638984 | tf_op jit(solution)/shard_map/ppermute | solution.py:379
  49.8 2.1 %collective-permute-done.4.inner = f32[13,32,128]{2,1,0:T(8,128)S(1)} collective-permute-done((f32[13,32,128]{2,1,0:T(8,128)S(1)}, f32[13,32,128]{2,1,0:T(8,128)S(1)}, u32[]{:S(2)}, u32[]{:S(2)}) %collective-permute-start.4) | collective-permute-done | bytes 213024 | tf_op jit(solution)/shard_map/ppermute | solution.py:380
  51.9 13.2 %collective-permute-done.5.outer = f32[13,32,128]{2,1,0:T(8,128)S(1)} collective-permute-done((f32[13,32,128]{2,1,0:T(8,128)S(1)}, f32[13,32,128]{2,1,0:T(8,128)S(1)}, u32[]{:S(2)}, u32[]{:S(2)}) %collective-permute-start.5) | collective-permute-done | bytes 213024 | tf_op jit(solution)/shard_map/ppermute | solution.py:379
  65.1 0.4 meridional.2
  65.5 0.1 collective-permute-start.6
  65.6 0.6 collective-permute-start.7
  66.1 3.4 %collective-permute-start.8 = (f32[4,3,16,128]{3,2,1,0:T(8,128)S(1)}, f32[4,3,16,128]{3,2,1,0:T(8,128)S(1)}, u32[]{:S(2)}, u32[]{:S(2)}) collective-permute-start(f32[4,3,16,128]{3,2,1,0:T(8,128)S(1)} %get-tuple-element.34), channel_id=1, source_target_pairs={{1,0},{2,1},{3,2},{4,3},{5,4},{6,5},{7,6},{8,7},{9,8},{10,9},{11,1... | collective-permute-start | bytes 294920 | tf_op jit(solution)/shard_map/ppermute | solution.py:373
  69.5 0.4 collective-permute-start.9
  69.9 1.8 %collective-permute-done.6.refs_0_ = f32[4,3,16,128]{3,2,1,0:T(8,128)S(1)} collective-permute-done((f32[4,3,16,128]{3,2,1,0:T(8,128)S(1)}, f32[4,3,16,128]{3,2,1,0:T(8,128)S(1)}, u32[]{:S(2)}, u32[]{:S(2)}) %collective-permute-start.6) | collective-permute-done | bytes 98336 | tf_op jit(solution)/shard_map/ppermute | solution.py:373
  71.7 1.1 %collective-permute-done.7.refs_1_ = f32[4,3,16,128]{3,2,1,0:T(8,128)S(1)} collective-permute-done((f32[4,3,16,128]{3,2,1,0:T(8,128)S(1)}, f32[4,3,16,128]{3,2,1,0:T(8,128)S(1)}, u32[]{:S(2)}, u32[]{:S(2)}) %collective-permute-start.7) | collective-permute-done | bytes 98336 | tf_op jit(solution)/shard_map/ppermute | solution.py:373
  72.8 0.0 collective-permute-done.8.refs_2_
  72.8 2.2 %collective-permute-done.9.refs_3_ = f32[4,3,16,128]{3,2,1,0:T(8,128)S(1)} collective-permute-done((f32[4,3,16,128]{3,2,1,0:T(8,128)S(1)}, f32[4,3,16,128]{3,2,1,0:T(8,128)S(1)}, u32[]{:S(2)}, u32[]{:S(2)}) %collective-permute-start.9) | collective-permute-done | bytes 98336 | tf_op jit(solution)/shard_map/ppermute | solution.py:373
  75.0 0.4 zonal.3
  75.3 0.1 collective-permute-start.10
  75.4 1.9 %collective-permute-start.11 = (f32[13,32,128]{2,1,0:T(8,128)S(1)}, f32[13,32,128]{2,1,0:T(8,128)S(1)}, u32[]{:S(2)}, u32[]{:S(2)}) collective-permute-start(f32[13,32,128]{2,1,0:T(8,128)S(1)} %get-tuple-element.38), channel_id=1, source_target_pairs={{0,0},{32,64},{64,32},{96,128},{128,96},{160,192},{192,160},{224,2... | collective-permute-start | bytes 638984 | tf_op jit(solution)/shard_map/ppermute | solution.py:379
  77.4 3.9 %collective-permute-done.10.inner = f32[13,32,128]{2,1,0:T(8,128)S(1)} collective-permute-done((f32[13,32,128]{2,1,0:T(8,128)S(1)}, f32[13,32,128]{2,1,0:T(8,128)S(1)}, u32[]{:S(2)}, u32[]{:S(2)}) %collective-permute-start.10) | collective-permute-done | bytes 213024 | tf_op jit(solution)/shard_map/ppermute | solution.py:380
  81.3 8.8 %collective-permute-done.11.outer = f32[13,32,128]{2,1,0:T(8,128)S(1)} collective-permute-done((f32[13,32,128]{2,1,0:T(8,128)S(1)}, f32[13,32,128]{2,1,0:T(8,128)S(1)}, u32[]{:S(2)}, u32[]{:S(2)}) %collective-permute-start.11) | collective-permute-done | bytes 213024 | tf_op jit(solution)/shard_map/ppermute | solution.py:379
  90.1 1.1 %meridional.3 = f32[4,4,32,128]{3,2,1,0:T(8,128)} custom-call(f32[4,4,32,128]{3,2,1,0:T(8,128)S(1)} %get-tuple-element.36.block, f32[32,1,128]{2,1,0:T(1,128)S(1)} %all_to_all.5.wind, f32[13,32,128]{2,1,0:T(8,128)S(1)} %collective-permute-done.10.inner, f32[13,32,128]{2,1,0:T(8,128)S(1)} %collective-permute-done.11.outer), custom_call_target="tpu_custom_call" | custom-call | tf_op jit(solution)/shard_map/meridional/pallas_call | solution.py:326
Async XLA Ops:
  8.0 35.4 %collective-permute-start = (f32[4,3,16,128]{3,2,1,0:T(8,128)}, f32[4,3,16,128]{3,2,1,0:T(8,128)S(1)}, u32[]{:S(2)}, u32[]{:S(2)}) collective-permute-start(f32[4,3,16,128]{3,2,1,0:T(8,128)} %get-tuple-element.24), channel_id=1, source_target_pairs={{0,1},{1,2},{2,3},{3,4},{4,5},{5,6},{6,7},{7,8},{8,9},{9,10},{10,1... | collective-permute-start | bytes 294920 | tf_op jit(solution)/shard_map/ppermute | solution.py:373
  8.1 35.3 %collective-permute-start.1 = (f32[4,3,16,128]{3,2,1,0:T(8,128)}, f32[4,3,16,128]{3,2,1,0:T(8,128)S(1)}, u32[]{:S(2)}, u32[]{:S(2)}) collective-permute-start(f32[4,3,16,128]{3,2,1,0:T(8,128)} %get-tuple-element.25), channel_id=1, source_target_pairs={{0,1},{1,2},{2,3},{3,4},{4,5},{5,6},{6,7},{7,8},{8,9},{9,10},{10,1... | collective-permute-start | bytes 294920 | tf_op jit(solution)/shard_map/ppermute | solution.py:373
  9.7 33.7 %collective-permute-start.2 = (f32[4,3,16,128]{3,2,1,0:T(8,128)}, f32[4,3,16,128]{3,2,1,0:T(8,128)S(1)}, u32[]{:S(2)}, u32[]{:S(2)}) collective-permute-start(f32[4,3,16,128]{3,2,1,0:T(8,128)} %get-tuple-element.26), channel_id=1, source_target_pairs={{1,0},{2,1},{3,2},{4,3},{5,4},{6,5},{7,6},{8,7},{9,8},{10,9},{11,1... | collective-permute-start | bytes 294920 | tf_op jit(solution)/shard_map/ppermute | solution.py:373
  12.0 31.4 %collective-permute-start.3 = (f32[4,3,16,128]{3,2,1,0:T(8,128)}, f32[4,3,16,128]{3,2,1,0:T(8,128)S(1)}, u32[]{:S(2)}, u32[]{:S(2)}) collective-permute-start(f32[4,3,16,128]{3,2,1,0:T(8,128)} %get-tuple-element.27), channel_id=1, source_target_pairs={{1,0},{2,1},{3,2},{4,3},{5,4},{6,5},{7,6},{8,7},{9,8},{10,9},{11,1... | collective-permute-start | bytes 294920 | tf_op jit(solution)/shard_map/ppermute | solution.py:373
  43.4 1.0 %copy-start = (f32[4,4,32,128]{3,2,1,0:T(8,128)S(1)}, f32[4,4,32,128]{3,2,1,0:T(8,128)}, u32[]{:S(2)}) copy-start(f32[4,4,32,128]{3,2,1,0:T(8,128)} %get-tuple-element.22.block) | copy-start | bytes 786436
  44.8 7.1 %collective-permute-start.4 = (f32[13,32,128]{2,1,0:T(8,128)S(1)}, f32[13,32,128]{2,1,0:T(8,128)S(1)}, u32[]{:S(2)}, u32[]{:S(2)}) collective-permute-start(f32[13,32,128]{2,1,0:T(8,128)S(1)} %get-tuple-element.29), channel_id=1, source_target_pairs={{0,32},{32,0},{64,96},{96,64},{128,160},{160,128},{192,224},{224,1... | collective-permute-start | bytes 638984 | tf_op jit(solution)/shard_map/ppermute | solution.py:380
  45.8 19.3 %collective-permute-start.5 = (f32[13,32,128]{2,1,0:T(8,128)S(1)}, f32[13,32,128]{2,1,0:T(8,128)S(1)}, u32[]{:S(2)}, u32[]{:S(2)}) collective-permute-start(f32[13,32,128]{2,1,0:T(8,128)S(1)} %get-tuple-element.30), channel_id=1, source_target_pairs={{0,0},{32,64},{64,32},{96,128},{128,96},{160,192},{192,160},{224,2... | collective-permute-start | bytes 638984 | tf_op jit(solution)/shard_map/ppermute | solution.py:379
  65.5 6.2 %collective-permute-start.6 = (f32[4,3,16,128]{3,2,1,0:T(8,128)S(1)}, f32[4,3,16,128]{3,2,1,0:T(8,128)S(1)}, u32[]{:S(2)}, u32[]{:S(2)}) collective-permute-start(f32[4,3,16,128]{3,2,1,0:T(8,128)S(1)} %get-tuple-element.32), channel_id=1, source_target_pairs={{0,1},{1,2},{2,3},{3,4},{4,5},{5,6},{6,7},{7,8},{8,9},{9,10},{10,1... | collective-permute-start | bytes 294920 | tf_op jit(solution)/shard_map/ppermute | solution.py:373
  65.6 7.2 %collective-permute-start.7 = (f32[4,3,16,128]{3,2,1,0:T(8,128)S(1)}, f32[4,3,16,128]{3,2,1,0:T(8,128)S(1)}, u32[]{:S(2)}, u32[]{:S(2)}) collective-permute-start(f32[4,3,16,128]{3,2,1,0:T(8,128)S(1)} %get-tuple-element.33), channel_id=1, source_target_pairs={{0,1},{1,2},{2,3},{3,4},{4,5},{5,6},{6,7},{7,8},{8,9},{9,10},{10,1... | collective-permute-start | bytes 294920 | tf_op jit(solution)/shard_map/ppermute | solution.py:373
  66.1 6.6 %collective-permute-start.8 = (f32[4,3,16,128]{3,2,1,0:T(8,128)S(1)}, f32[4,3,16,128]{3,2,1,0:T(8,128)S(1)}, u32[]{:S(2)}, u32[]{:S(2)}) collective-permute-start(f32[4,3,16,128]{3,2,1,0:T(8,128)S(1)} %get-tuple-element.34), channel_id=1, source_target_pairs={{1,0},{2,1},{3,2},{4,3},{5,4},{6,5},{7,6},{8,7},{9,8},{10,9},{11,1... | collective-permute-start | bytes 294920 | tf_op jit(solution)/shard_map/ppermute | solution.py:373
  69.5 5.5 %collective-permute-start.9 = (f32[4,3,16,128]{3,2,1,0:T(8,128)S(1)}, f32[4,3,16,128]{3,2,1,0:T(8,128)S(1)}, u32[]{:S(2)}, u32[]{:S(2)}) collective-permute-start(f32[4,3,16,128]{3,2,1,0:T(8,128)S(1)} %get-tuple-element.35), channel_id=1, source_target_pairs={{1,0},{2,1},{3,2},{4,3},{5,4},{6,5},{7,6},{8,7},{9,8},{10,9},{11,1... | collective-permute-start | bytes 294920 | tf_op jit(solution)/shard_map/ppermute | solution.py:373
  75.3 5.9 %collective-permute-start.10 = (f32[13,32,128]{2,1,0:T(8,128)S(1)}, f32[13,32,128]{2,1,0:T(8,128)S(1)}, u32[]{:S(2)}, u32[]{:S(2)}) collective-permute-start(f32[13,32,128]{2,1,0:T(8,128)S(1)} %get-tuple-element.37), channel_id=1, source_target_pairs={{0,32},{32,0},{64,96},{96,64},{128,160},{160,128},{192,224},{224,1... | collective-permute-start | bytes 638984 | tf_op jit(solution)/shard_map/ppermute | solution.py:380
  75.4 14.6 %collective-permute-start.11 = (f32[13,32,128]{2,1,0:T(8,128)S(1)}, f32[13,32,128]{2,1,0:T(8,128)S(1)}, u32[]{:S(2)}, u32[]{:S(2)}) collective-permute-start(f32[13,32,128]{2,1,0:T(8,128)S(1)} %get-tuple-element.38), channel_id=1, source_target_pairs={{0,0},{32,64},{64,32},{96,128},{128,96},{160,192},{192,160},{224,2... | collective-permute-start | bytes 638984 | tf_op jit(solution)/shard_map/ppermute | solution.py:379

commit v2 on v1

--- a/solution.py
+++ b/solution.py
@@ -11,7 +11,7 @@
 LANES = 16
 FLOOR = 1e-30
 GROUP = 8
-UNROLL = 2
+UNROLL = 4
 SHUFFLED = 1
 PARTS = 2
 INPUTS = 8
@@ -203,11 +203,11 @@
     n_lat, n_lon, levels, kinds = species.shape
     reactions, longitudes = recipe.shape[1], eastward.shape[2]
     columns = n_lat * n_lon
-    halo = jax.ShapeDtypeStruct((n_lat, n_lon - 1, levels // PARTS, kinds), F32)
+    halo = pltpu.VMEM((n_lat, n_lon - 1, levels // PARTS, kinds), F32)
     return pl.pallas_call(
         functools.partial(chemistry_kernel, group=GROUP),
         out_shape=(
-            jax.ShapeDtypeStruct(species.shape, F32),
+            pltpu.VMEM(species.shape, F32),
             jax.ShapeDtypeStruct((longitudes // n_lon, 1, 128), F32),
         )
         + (halo,) * (2 * PARTS),
@@ -225,7 +225,7 @@
             pltpu.VMEM((columns * levels // 2, 2 * kinds), F32),
             pltpu.SemaphoreType.DMA((INPUTS,)),
         ],
-        compiler_params=pltpu.CompilerParams(vmem_limit_bytes=62 << 20),
+        compiler_params=pltpu.CompilerParams(vmem_limit_bytes=60 << 20),
         cost_estimate=pl.CostEstimate(
             flops=int(2e10), bytes_accessed=2 << 20, transcendentals=0
         ),
@@ -292,7 +292,7 @@
                 outer[at] = jnp.where(even, below, value)
 
 
-def meridional_kernel(block, wind, inner, outer, swept, *refs):
+def meridional_kernel(block, wind, outer, inner, swept, *refs):
     *sends, rows = refs
     n_lat, n_lon = block.shape[:2]
     tile = block.shape[2:]
@@ -376,12 +376,12 @@
         block, inner, outer = sweep(
             zonal_kernel, block, wind, halos, (meridional_halo,) * 2, "zonal"
         )
+        inner = lax.ppermute(inner, "lat", inner_pairs)
         outer = lax.ppermute(outer, "lat", outer_pairs)
-        inner = lax.ppermute(inner, "lat", inner_pairs)
         last = step == ADV_STEPS - 1
         sent_shapes = () if last else (zonal_halo,) * (2 * PARTS)
         block, *sends = sweep(
-            meridional_kernel, block, wind, (inner, outer), sent_shapes, "meridional"
+            meridional_kernel, block, wind, (outer, inner), sent_shapes, "meridional"
         )
     return block
 

time: 91.1 us -> 88.1 us (0.967)
  blocking collectives: 31 us -> 29.1 us
  local copies, waits for them, and re-layouts: 0.95 us -> 0 us
    ppermute x2, waiting for transfers between devices: 6 us -> 0.01 us  [per_device(): inner = lax.ppermute(inner, 'lat', inner_pairs)]
    ppermute x2, waiting for transfers between devices: 22 us -> 27 us  [per_device(): outer = lax.ppermute(outer, 'lat', outer_pairs)]
    all_to_all x1, blocking collectives: 31 us -> 29.1 us  [per_device(): lax.all_to_all(packed, 'lon', split_axis=0, concat_axis=0, tiled=True)]
    unnamed x2 -> x0, local copies, waits for them, and re-layouts: 0.95 us -> none
  transfers between devices with their start and end apart: 12 -> 12, of which waited for: 7 -> 5; matrix products, arithmetic and copies ran while one was open for 0% -> 0% of each run, Pallas kernels for 0% -> 0%
where the time goes in v2:
time: 88.1 us; the launch traced here: 88.5 us
  waiting for transfers between devices  32.1 us (36%)
  blocking collectives  29.1 us (33%)
  starting transfers between devices  16 us (18%)
  Pallas kernels  11.2 us (13%)
    all_to_all x1, blocking collectives, per_device(): lax.all_to_all(packed, 'lon', split_axis=0, concat_axis=0, tiled=True)  29.1 us
    ppermute x2, waiting for transfers between devices, per_device(): outer = lax.ppermute(outer, 'lat', outer_pairs)  27 us
    pallas_call x1, Pallas kernels, chemistry(): pl.pallas_call(functools.partial(chemistry_kernel, group=GROUP), out_shap...  8.9 us
    ppermute x8, starting transfers between devices, per_device(): lax.ppermute(sent, 'lon', eastbound if i < PARTS else westbound)  8.87 us
    ppermute x2, starting transfers between devices, per_device(): outer = lax.ppermute(outer, 'lat', outer_pairs)  6.05 us
    ppermute x8, waiting for transfers between devices, per_device(): lax.ppermute(sent, 'lon', eastbound if i < PARTS else westbound)  5.09 us
    pallas_call x4, Pallas kernels, sweep(): pl.pallas_call(kernel, out_shape=tuple((jax.ShapeDtypeStruct(shape, F32)...  2.27 us
  transfers between devices with their start and end apart: 12, of which 5 were waited for; matrix products, arithmetic and copies ran while one was open for 0% of the time, Pallas kernels for 0%

profile of v2, /device:TPU:192, one launch (start us, length us, event | category | flops | bytes accessed | tf_op | source)
XLA Modules:
  0.0 88.5 jit_solution(15221377243252435531)
XLA Ops:
  0.0 8.9 %chemistry.1 = (f32[4,4,32,128]{3,2,1,0:T(8,128)S(1)}, f32[32,1,128]{2,1,0:T(1,128)}, f32[4,3,16,128]{3,2,1,0:T(8,128)S(1)}, f32[4,3,16,128]{3,2,1,0:T(8,128)S(1...) custom-call(s32[4,4]{1,0:T(4,128)} %counts.1, f32[4,4]{1,0:T(4,128)} %solar.1, s32[4,512]{1,0:T(4,128)} %refs_0_.1, ...), custom_call_target="tpu_custom_call" | custom-call | flops 20000000000 | bytes 2097152 | tf_op jit(solution)/shard_map/chemistry/pallas_call | solution.py:207
  8.9 0.1 collective-permute-start
  9.0 1.6 %collective-permute-start.1 = (f32[4,3,16,128]{3,2,1,0:T(8,128)S(1)}, f32[4,3,16,128]{3,2,1,0:T(8,128)S(1)}, u32[]{:S(2)}, u32[]{:S(2)}) collective-permute-start(f32[4,3,16,128]{3,2,1,0:T(8,128)S(1)} %get-tuple-element.25), channel_id=1, source_target_pairs={{0,1},{1,2},{2,3},{3,4},{4,5},{5,6},{6,7},{7,8},{8,9},{9,10},{10,1... | collective-permute-start | bytes 294920 | tf_op jit(solution)/shard_map/ppermute | solution.py:373
  10.6 2.3 %collective-permute-start.2 = (f32[4,3,16,128]{3,2,1,0:T(8,128)S(1)}, f32[4,3,16,128]{3,2,1,0:T(8,128)S(1)}, u32[]{:S(2)}, u32[]{:S(2)}) collective-permute-start(f32[4,3,16,128]{3,2,1,0:T(8,128)S(1)} %get-tuple-element.26), channel_id=1, source_target_pairs={{1,0},{2,1},{3,2},{4,3},{5,4},{6,5},{7,6},{8,7},{9,8},{10,9},{11,1... | collective-permute-start | bytes 294920 | tf_op jit(solution)/shard_map/ppermute | solution.py:373
  12.9 0.4 collective-permute-start.3
  13.4 29.1 %all_to_all.5.wind = f32[32,1,128]{2,1,0:T(1,128)S(1)} all-to-all(f32[32,1,128]{2,1,0:T(1,128)} %get-tuple-element.23), channel_id=1, replica_groups=mesh['lat'=8,'lon'=32] {'lon'}, dimensions={0} | all-to-all | bytes 32768 | tf_op jit(solution)/shard_map/all_to_all | solution.py:368
  42.5 0.0 collective-permute-done.refs_0_
  42.5 0.0 collective-permute-done.1.refs_1_
  42.5 0.0 collective-permute-done.2.refs_2_
  42.5 0.0 collective-permute-done.3.refs_3_
  42.5 0.4 zonal.2
  42.9 4.1 %collective-permute-start.4 = (f32[13,32,128]{2,1,0:T(8,128)S(1)}, f32[13,32,128]{2,1,0:T(8,128)S(1)}, u32[]{:S(2)}, u32[]{:S(2)}) collective-permute-start(f32[13,32,128]{2,1,0:T(8,128)S(1)} %get-tuple-element.29), channel_id=1, source_target_pairs={{0,0},{32,64},{64,32},{96,128},{128,96},{160,192},{192,160},{224,2... | collective-permute-start | bytes 638984 | tf_op jit(solution)/shard_map/ppermute | solution.py:380
  47.0 1.0 %collective-permute-start.5 = (f32[13,32,128]{2,1,0:T(8,128)S(1)}, f32[13,32,128]{2,1,0:T(8,128)S(1)}, u32[]{:S(2)}, u32[]{:S(2)}) collective-permute-start(f32[13,32,128]{2,1,0:T(8,128)S(1)} %get-tuple-element.30), channel_id=1, source_target_pairs={{0,32},{32,0},{64,96},{96,64},{128,160},{160,128},{192,224},{224,1... | collective-permute-start | bytes 638984 | tf_op jit(solution)/shard_map/ppermute | solution.py:379
  48.0 14.4 %collective-permute-done.4.outer = f32[13,32,128]{2,1,0:T(8,128)S(1)} collective-permute-done((f32[13,32,128]{2,1,0:T(8,128)S(1)}, f32[13,32,128]{2,1,0:T(8,128)S(1)}, u32[]{:S(2)}, u32[]{:S(2)}) %collective-permute-start.4) | collective-permute-done | bytes 213024 | tf_op jit(solution)/shard_map/ppermute | solution.py:380
  62.4 0.0 collective-permute-done.5.inner
  62.4 0.4 meridional.2
  62.8 0.1 collective-permute-start.6
  62.9 0.7 collective-permute-start.7
  63.6 3.3 %collective-permute-start.8 = (f32[4,3,16,128]{3,2,1,0:T(8,128)S(1)}, f32[4,3,16,128]{3,2,1,0:T(8,128)S(1)}, u32[]{:S(2)}, u32[]{:S(2)}) collective-permute-start(f32[4,3,16,128]{3,2,1,0:T(8,128)S(1)} %get-tuple-element.34), channel_id=1, source_target_pairs={{1,0},{2,1},{3,2},{4,3},{5,4},{6,5},{7,6},{8,7},{9,8},{10,9},{11,1... | collective-permute-start | bytes 294920 | tf_op jit(solution)/shard_map/ppermute | solution.py:373
  66.8 0.4 collective-permute-start.9
  67.3 1.8 %collective-permute-done.6.refs_0_ = f32[4,3,16,128]{3,2,1,0:T(8,128)S(1)} collective-permute-done((f32[4,3,16,128]{3,2,1,0:T(8,128)S(1)}, f32[4,3,16,128]{3,2,1,0:T(8,128)S(1)}, u32[]{:S(2)}, u32[]{:S(2)}) %collective-permute-start.6) | collective-permute-done | bytes 98336 | tf_op jit(solution)/shard_map/ppermute | solution.py:373
  69.0 1.1 %collective-permute-done.7.refs_1_ = f32[4,3,16,128]{3,2,1,0:T(8,128)S(1)} collective-permute-done((f32[4,3,16,128]{3,2,1,0:T(8,128)S(1)}, f32[4,3,16,128]{3,2,1,0:T(8,128)S(1)}, u32[]{:S(2)}, u32[]{:S(2)}) %collective-permute-start.7) | collective-permute-done | bytes 98336 | tf_op jit(solution)/shard_map/ppermute | solution.py:373
  70.1 0.0 collective-permute-done.8.refs_2_
  70.1 2.2 %collective-permute-done.9.refs_3_ = f32[4,3,16,128]{3,2,1,0:T(8,128)S(1)} collective-permute-done((f32[4,3,16,128]{3,2,1,0:T(8,128)S(1)}, f32[4,3,16,128]{3,2,1,0:T(8,128)S(1)}, u32[]{:S(2)}, u32[]{:S(2)}) %collective-permute-start.9) | collective-permute-done | bytes 98336 | tf_op jit(solution)/shard_map/ppermute | solution.py:373
  72.3 0.4 zonal.3
  72.7 1.9 %collective-permute-start.10 = (f32[13,32,128]{2,1,0:T(8,128)S(1)}, f32[13,32,128]{2,1,0:T(8,128)S(1)}, u32[]{:S(2)}, u32[]{:S(2)}) collective-permute-start(f32[13,32,128]{2,1,0:T(8,128)S(1)} %get-tuple-element.37), channel_id=1, source_target_pairs={{0,0},{32,64},{64,32},{96,128},{128,96},{160,192},{192,160},{224,2... | collective-permute-start | bytes 638984 | tf_op jit(solution)/shard_map/ppermute | solution.py:380
  74.7 0.1 collective-permute-start.11
  74.8 12.7 %collective-permute-done.10.outer = f32[13,32,128]{2,1,0:T(8,128)S(1)} collective-permute-done((f32[13,32,128]{2,1,0:T(8,128)S(1)}, f32[13,32,128]{2,1,0:T(8,128)S(1)}, u32[]{:S(2)}, u32[]{:S(2)}) %collective-permute-start.10) | collective-permute-done | bytes 213024 | tf_op jit(solution)/shard_map/ppermute | solution.py:380
  87.4 0.0 collective-permute-done.11.inner
  87.4 1.1 %meridional.3 = f32[4,4,32,128]{3,2,1,0:T(8,128)} custom-call(f32[4,4,32,128]{3,2,1,0:T(8,128)S(1)} %get-tuple-element.36.block, f32[32,1,128]{2,1,0:T(1,128)S(1)} %all_to_all.5.wind, f32[13,32,128]{2,1,0:T(8,128)S(1)} %collective-permute-done.10.outer, f32[13,32,128]{2,1,0:T(8,128)S(1)} %collective-permute-done.11.inner), custom_call_target="tpu_custom_call" | custom-call | tf_op jit(solution)/shard_map/meridional/pallas_call | solution.py:326
Async XLA Ops:
  8.9 33.6 %collective-permute-start = (f32[4,3,16,128]{3,2,1,0:T(8,128)S(1)}, f32[4,3,16,128]{3,2,1,0:T(8,128)S(1)}, u32[]{:S(2)}, u32[]{:S(2)}) collective-permute-start(f32[4,3,16,128]{3,2,1,0:T(8,128)S(1)} %get-tuple-element.24), channel_id=1, source_target_pairs={{0,1},{1,2},{2,3},{3,4},{4,5},{5,6},{6,7},{7,8},{8,9},{9,10},{10,1... | collective-permute-start | bytes 294920 | tf_op jit(solution)/shard_map/ppermute | solution.py:373
  9.0 33.5 %collective-permute-start.1 = (f32[4,3,16,128]{3,2,1,0:T(8,128)S(1)}, f32[4,3,16,128]{3,2,1,0:T(8,128)S(1)}, u32[]{:S(2)}, u32[]{:S(2)}) collective-permute-start(f32[4,3,16,128]{3,2,1,0:T(8,128)S(1)} %get-tuple-element.25), channel_id=1, source_target_pairs={{0,1},{1,2},{2,3},{3,4},{4,5},{5,6},{6,7},{7,8},{8,9},{9,10},{10,1... | collective-permute-start | bytes 294920 | tf_op jit(solution)/shard_map/ppermute | solution.py:373
  10.6 31.9 %collective-permute-start.2 = (f32[4,3,16,128]{3,2,1,0:T(8,128)S(1)}, f32[4,3,16,128]{3,2,1,0:T(8,128)S(1)}, u32[]{:S(2)}, u32[]{:S(2)}) collective-permute-start(f32[4,3,16,128]{3,2,1,0:T(8,128)S(1)} %get-tuple-element.26), channel_id=1, source_target_pairs={{1,0},{2,1},{3,2},{4,3},{5,4},{6,5},{7,6},{8,7},{9,8},{10,9},{11,1... | collective-permute-start | bytes 294920 | tf_op jit(solution)/shard_map/ppermute | solution.py:373
  12.9 29.6 %collective-permute-start.3 = (f32[4,3,16,128]{3,2,1,0:T(8,128)S(1)}, f32[4,3,16,128]{3,2,1,0:T(8,128)S(1)}, u32[]{:S(2)}, u32[]{:S(2)}) collective-permute-start(f32[4,3,16,128]{3,2,1,0:T(8,128)S(1)} %get-tuple-element.27), channel_id=1, source_target_pairs={{1,0},{2,1},{3,2},{4,3},{5,4},{6,5},{7,6},{8,7},{9,8},{10,9},{11,1... | collective-permute-start | bytes 294920 | tf_op jit(solution)/shard_map/ppermute | solution.py:373
  42.9 19.5 %collective-permute-start.4 = (f32[13,32,128]{2,1,0:T(8,128)S(1)}, f32[13,32,128]{2,1,0:T(8,128)S(1)}, u32[]{:S(2)}, u32[]{:S(2)}) collective-permute-start(f32[13,32,128]{2,1,0:T(8,128)S(1)} %get-tuple-element.29), channel_id=1, source_target_pairs={{0,0},{32,64},{64,32},{96,128},{128,96},{160,192},{192,160},{224,2... | collective-permute-start | bytes 638984 | tf_op jit(solution)/shard_map/ppermute | solution.py:380
  47.0 15.4 %collective-permute-start.5 = (f32[13,32,128]{2,1,0:T(8,128)S(1)}, f32[13,32,128]{2,1,0:T(8,128)S(1)}, u32[]{:S(2)}, u32[]{:S(2)}) collective-permute-start(f32[13,32,128]{2,1,0:T(8,128)S(1)} %get-tuple-element.30), channel_id=1, source_target_pairs={{0,32},{32,0},{64,96},{96,64},{128,160},{160,128},{192,224},{224,1... | collective-permute-start | bytes 638984 | tf_op jit(solution)/shard_map/ppermute | solution.py:379
  62.8 6.2 %collective-permute-start.6 = (f32[4,3,16,128]{3,2,1,0:T(8,128)S(1)}, f32[4,3,16,128]{3,2,1,0:T(8,128)S(1)}, u32[]{:S(2)}, u32[]{:S(2)}) collective-permute-start(f32[4,3,16,128]{3,2,1,0:T(8,128)S(1)} %get-tuple-element.32), channel_id=1, source_target_pairs={{0,1},{1,2},{2,3},{3,4},{4,5},{5,6},{6,7},{7,8},{8,9},{9,10},{10,1... | collective-permute-start | bytes 294920 | tf_op jit(solution)/shard_map/ppermute | solution.py:373
  62.9 7.2 %collective-permute-start.7 = (f32[4,3,16,128]{3,2,1,0:T(8,128)S(1)}, f32[4,3,16,128]{3,2,1,0:T(8,128)S(1)}, u32[]{:S(2)}, u32[]{:S(2)}) collective-permute-start(f32[4,3,16,128]{3,2,1,0:T(8,128)S(1)} %get-tuple-element.33), channel_id=1, source_target_pairs={{0,1},{1,2},{2,3},{3,4},{4,5},{5,6},{6,7},{7,8},{8,9},{9,10},{10,1... | collective-permute-start | bytes 294920 | tf_op jit(solution)/shard_map/ppermute | solution.py:373
  63.6 6.5 %collective-permute-start.8 = (f32[4,3,16,128]{3,2,1,0:T(8,128)S(1)}, f32[4,3,16,128]{3,2,1,0:T(8,128)S(1)}, u32[]{:S(2)}, u32[]{:S(2)}) collective-permute-start(f32[4,3,16,128]{3,2,1,0:T(8,128)S(1)} %get-tuple-element.34), channel_id=1, source_target_pairs={{1,0},{2,1},{3,2},{4,3},{5,4},{6,5},{7,6},{8,7},{9,8},{10,9},{11,1... | collective-permute-start | bytes 294920 | tf_op jit(solution)/shard_map/ppermute | solution.py:373
  66.8 5.5 %collective-permute-start.9 = (f32[4,3,16,128]{3,2,1,0:T(8,128)S(1)}, f32[4,3,16,128]{3,2,1,0:T(8,128)S(1)}, u32[]{:S(2)}, u32[]{:S(2)}) collective-permute-start(f32[4,3,16,128]{3,2,1,0:T(8,128)S(1)} %get-tuple-element.35), channel_id=1, source_target_pairs={{1,0},{2,1},{3,2},{4,3},{5,4},{6,5},{7,6},{8,7},{9,8},{10,9},{11,1... | collective-permute-start | bytes 294920 | tf_op jit(solution)/shard_map/ppermute | solution.py:373
  72.7 14.7 %collective-permute-start.10 = (f32[13,32,128]{2,1,0:T(8,128)S(1)}, f32[13,32,128]{2,1,0:T(8,128)S(1)}, u32[]{:S(2)}, u32[]{:S(2)}) collective-permute-start(f32[13,32,128]{2,1,0:T(8,128)S(1)} %get-tuple-element.37), channel_id=1, source_target_pairs={{0,0},{32,64},{64,32},{96,128},{128,96},{160,192},{192,160},{224,2... | collective-permute-start | bytes 638984 | tf_op jit(solution)/shard_map/ppermute | solution.py:380
  74.7 12.8 %collective-permute-start.11 = (f32[13,32,128]{2,1,0:T(8,128)S(1)}, f32[13,32,128]{2,1,0:T(8,128)S(1)}, u32[]{:S(2)}, u32[]{:S(2)}) collective-permute-start(f32[13,32,128]{2,1,0:T(8,128)S(1)} %get-tuple-element.38), channel_id=1, source_target_pairs={{0,32},{32,0},{64,96},{96,64},{128,160},{160,128},{192,224},{224,1... | collective-permute-start | bytes 638984 | tf_op jit(solution)/shard_map/ppermute | solution.py:379

commit v3 on v2

--- a/solution.py
+++ b/solution.py
@@ -275,8 +275,9 @@
     tile = block.shape[2:]
     winds = wind_rows(wind, rows)
     even = lax.rem(lax.axis_index("lat"), 2) == 0
-    inner[(n_lat - 1) * n_lon] = winds
-    outer[(n_lat - 1) * n_lon] = winds
+    if inner.shape[0] > (n_lat - 1) * n_lon:
+        inner[(n_lat - 1) * n_lon] = winds
+        outer[(n_lat - 1) * n_lon] = winds
     lines = []
     for a in range(n_lat):
         cells = [load_parts(low, (a, i)) for i in range(3)]
@@ -292,8 +293,13 @@
                 outer[at] = jnp.where(even, below, value)
 
 
-def meridional_kernel(block, wind, outer, inner, swept, *refs):
-    *sends, rows = refs
+def meridional_kernel(block, wind, outer, inner, *refs):
+    *refs, rows = refs
+    first = inner.shape[0] > 3 * block.shape[1]
+    if first:
+        swept, passed, *sends = refs
+    else:
+        given, swept, sends = *refs, ()
     n_lat, n_lon = block.shape[:2]
     tile = block.shape[2:]
     band = lax.axis_index("lat")
@@ -306,7 +312,10 @@
     def high(at):
         return jnp.where(north_end, 0.0, jnp.where(even, inner[at], outer[at]))
 
-    winds, above = wind_rows(wind, rows), high(3 * n_lon)
+    winds = wind_rows(wind, rows)
+    above = high(3 * n_lon) if first else given[...]
+    if first:
+        passed[...] = above
     for i in range(n_lon):
         cells = [low(a * n_lon + i) for a in range(3)]
         cells += [block[a, i] for a in range(n_lat)]
@@ -367,22 +376,24 @@
     )
     wind = lax.all_to_all(packed, "lon", split_axis=0, concat_axis=0, tiled=True)
     zonal_halo = (n_lat, n_lon - 1, levels // PARTS, kinds)
-    meridional_halo = ((n_lat - 1) * n_lon + 1, levels, kinds)
+    rows = (n_lat - 1) * n_lon
+    above = ()
     for step in range(ADV_STEPS):
         halos = [
             lax.ppermute(sent, "lon", eastbound if i < PARTS else westbound)
             for i, sent in enumerate(sends)
         ]
+        meridional_halo = (rows + (step == 0), levels, kinds)
         block, inner, outer = sweep(
             zonal_kernel, block, wind, halos, (meridional_halo,) * 2, "zonal"
         )
         inner = lax.ppermute(inner, "lat", inner_pairs)
         outer = lax.ppermute(outer, "lat", outer_pairs)
-        last = step == ADV_STEPS - 1
-        sent_shapes = () if last else (zonal_halo,) * (2 * PARTS)
+        sent_shapes = () if step else ((levels, 128),) + (zonal_halo,) * (2 * PARTS)
         block, *sends = sweep(
-            meridional_kernel, block, wind, (outer, inner), sent_shapes, "meridional"
+            meridional_kernel, block, wind, (outer, inner, *above), sent_shapes, "meridional"
         )
+        above, sends = sends[:1], sends[1:]
     return block
 
 

time: 88.1 us -> 88.3 us (level); the launches traced: 88.5 us -> 87.8 us
  no operation moved by 1% of the time
where the time goes in v3:
time: 88.3 us; the launch traced here: 87.8 us
  waiting for transfers between devices  31.4 us (36%)
  blocking collectives  29.1 us (33%)
  starting transfers between devices  16.1 us (18%)
  Pallas kernels  11.2 us (13%)
    all_to_all x1, blocking collectives, per_device(): lax.all_to_all(packed, 'lon', split_axis=0, concat_axis=0, tiled=True)  29.1 us
    ppermute x2, waiting for transfers between devices, per_device(): outer = lax.ppermute(outer, 'lat', outer_pairs)  26.4 us
    pallas_call x1, Pallas kernels, chemistry(): pl.pallas_call(functools.partial(chemistry_kernel, group=GROUP), out_shap...  8.9 us
    ppermute x8, starting transfers between devices, per_device(): lax.ppermute(sent, 'lon', eastbound if i < PARTS else westbound)  8.87 us
    ppermute x2, starting transfers between devices, per_device(): outer = lax.ppermute(outer, 'lat', outer_pairs)  6.03 us
    ppermute x8, waiting for transfers between devices, per_device(): lax.ppermute(sent, 'lon', eastbound if i < PARTS else westbound)  4.92 us
    pallas_call x4, Pallas kernels, sweep(): pl.pallas_call(kernel, out_shape=tuple((jax.ShapeDtypeStruct(shape, F32)...  2.28 us
  transfers between devices with their start and end apart: 12, of which 5 were waited for; matrix products, arithmetic and copies ran while one was open for 0% of the time, Pallas kernels for 0%

profile of v3, /device:TPU:192, one launch (start us, length us, event | category | flops | bytes accessed | tf_op | source)
XLA Modules:
  0.0 87.8 jit_solution(4650910139692955897)
XLA Ops:
  0.0 8.9 %chemistry.1 = (f32[4,4,32,128]{3,2,1,0:T(8,128)S(1)}, f32[32,1,128]{2,1,0:T(1,128)}, f32[4,3,16,128]{3,2,1,0:T(8,128)S(1)}, f32[4,3,16,128]{3,2,1,0:T(8,128)S(1...) custom-call(s32[4,4]{1,0:T(4,128)} %counts.1, f32[4,4]{1,0:T(4,128)} %solar.1, s32[4,512]{1,0:T(4,128)} %refs_0_.1, ...), custom_call_target="tpu_custom_call" | custom-call | flops 20000000000 | bytes 2097152 | tf_op jit(solution)/shard_map/chemistry/pallas_call | solution.py:207
  8.9 0.1 collective-permute-start
  9.0 1.6 %collective-permute-start.1 = (f32[4,3,16,128]{3,2,1,0:T(8,128)S(1)}, f32[4,3,16,128]{3,2,1,0:T(8,128)S(1)}, u32[]{:S(2)}, u32[]{:S(2)}) collective-permute-start(f32[4,3,16,128]{3,2,1,0:T(8,128)S(1)} %get-tuple-element.26), channel_id=1, source_target_pairs={{0,1},{1,2},{2,3},{3,4},{4,5},{5,6},{6,7},{7,8},{8,9},{9,10},{10,1... | collective-permute-start | bytes 294920 | tf_op jit(solution)/shard_map/ppermute | solution.py:383
  10.6 2.3 %collective-permute-start.2 = (f32[4,3,16,128]{3,2,1,0:T(8,128)S(1)}, f32[4,3,16,128]{3,2,1,0:T(8,128)S(1)}, u32[]{:S(2)}, u32[]{:S(2)}) collective-permute-start(f32[4,3,16,128]{3,2,1,0:T(8,128)S(1)} %get-tuple-element.27), channel_id=1, source_target_pairs={{1,0},{2,1},{3,2},{4,3},{5,4},{6,5},{7,6},{8,7},{9,8},{10,9},{11,1... | collective-permute-start | bytes 294920 | tf_op jit(solution)/shard_map/ppermute | solution.py:383
  12.9 0.4 collective-permute-start.3
  13.4 29.1 %all_to_all.5.wind = f32[32,1,128]{2,1,0:T(1,128)S(1)} all-to-all(f32[32,1,128]{2,1,0:T(1,128)} %get-tuple-element.24), channel_id=1, replica_groups=mesh['lat'=8,'lon'=32] {'lon'}, dimensions={0} | all-to-all | bytes 32768 | tf_op jit(solution)/shard_map/all_to_all | solution.py:377
  42.5 0.0 collective-permute-done.refs_0_
  42.5 0.0 collective-permute-done.1.refs_1_
  42.5 0.0 collective-permute-done.2.refs_2_
  42.5 0.0 collective-permute-done.3.refs_3_
  42.5 0.4 zonal.2
  42.9 4.0 %collective-permute-start.4 = (f32[13,32,128]{2,1,0:T(8,128)S(1)}, f32[13,32,128]{2,1,0:T(8,128)S(1)}, u32[]{:S(2)}, u32[]{:S(2)}) collective-permute-start(f32[13,32,128]{2,1,0:T(8,128)S(1)} %get-tuple-element.30), channel_id=1, source_target_pairs={{0,0},{32,64},{64,32},{96,128},{128,96},{160,192},{192,160},{224,2... | collective-permute-start | bytes 638984 | tf_op jit(solution)/shard_map/ppermute | solution.py:391
  47.0 1.1 %collective-permute-start.5 = (f32[13,32,128]{2,1,0:T(8,128)S(1)}, f32[13,32,128]{2,1,0:T(8,128)S(1)}, u32[]{:S(2)}, u32[]{:S(2)}) collective-permute-start(f32[13,32,128]{2,1,0:T(8,128)S(1)} %get-tuple-element.31), channel_id=1, source_target_pairs={{0,32},{32,0},{64,96},{96,64},{128,160},{160,128},{192,224},{224,1... | collective-permute-start | bytes 638984 | tf_op jit(solution)/shard_map/ppermute | solution.py:390
  48.0 14.4 %collective-permute-done.4.outer = f32[13,32,128]{2,1,0:T(8,128)S(1)} collective-permute-done((f32[13,32,128]{2,1,0:T(8,128)S(1)}, f32[13,32,128]{2,1,0:T(8,128)S(1)}, u32[]{:S(2)}, u32[]{:S(2)}) %collective-permute-start.4) | collective-permute-done | bytes 213024 | tf_op jit(solution)/shard_map/ppermute | solution.py:391
  62.4 0.0 collective-permute-done.5.inner
  62.4 0.4 meridional.2
  62.8 0.1 collective-permute-start.6
  62.9 0.7 collective-permute-start.7
  63.6 3.3 %collective-permute-start.8 = (f32[4,3,16,128]{3,2,1,0:T(8,128)S(1)}, f32[4,3,16,128]{3,2,1,0:T(8,128)S(1)}, u32[]{:S(2)}, u32[]{:S(2)}) collective-permute-start(f32[4,3,16,128]{3,2,1,0:T(8,128)S(1)} %get-tuple-element.35), channel_id=1, source_target_pairs={{1,0},{2,1},{3,2},{4,3},{5,4},{6,5},{7,6},{8,7},{9,8},{10,9},{11,1... | collective-permute-start | bytes 294920 | tf_op jit(solution)/shard_map/ppermute | solution.py:383
  66.8 0.4 collective-permute-start.9
  67.3 1.8 %collective-permute-done.6.refs_0_ = f32[4,3,16,128]{3,2,1,0:T(8,128)S(1)} collective-permute-done((f32[4,3,16,128]{3,2,1,0:T(8,128)S(1)}, f32[4,3,16,128]{3,2,1,0:T(8,128)S(1)}, u32[]{:S(2)}, u32[]{:S(2)}) %collective-permute-start.6) | collective-permute-done | bytes 98336 | tf_op jit(solution)/shard_map/ppermute | solution.py:383
  69.0 1.1 %collective-permute-done.7.refs_1_ = f32[4,3,16,128]{3,2,1,0:T(8,128)S(1)} collective-permute-done((f32[4,3,16,128]{3,2,1,0:T(8,128)S(1)}, f32[4,3,16,128]{3,2,1,0:T(8,128)S(1)}, u32[]{:S(2)}, u32[]{:S(2)}) %collective-permute-start.7) | collective-permute-done | bytes 98336 | tf_op jit(solution)/shard_map/ppermute | solution.py:383
  70.1 0.0 collective-permute-done.8.refs_2_
  70.1 2.1 %collective-permute-done.9.refs_3_ = f32[4,3,16,128]{3,2,1,0:T(8,128)S(1)} collective-permute-done((f32[4,3,16,128]{3,2,1,0:T(8,128)S(1)}, f32[4,3,16,128]{3,2,1,0:T(8,128)S(1)}, u32[]{:S(2)}, u32[]{:S(2)}) %collective-permute-start.9) | collective-permute-done | bytes 98336 | tf_op jit(solution)/shard_map/ppermute | solution.py:383
  72.2 0.4 zonal.3
  72.5 2.0 %collective-permute-start.10 = (f32[12,32,128]{2,1,0:T(8,128)S(1)}, f32[12,32,128]{2,1,0:T(8,128)S(1)}, u32[]{:S(2)}, u32[]{:S(2)}) collective-permute-start(f32[12,32,128]{2,1,0:T(8,128)S(1)} %get-tuple-element.38), channel_id=1, source_target_pairs={{0,0},{32,64},{64,32},{96,128},{128,96},{160,192},{192,160},{224,2... | collective-permute-start | bytes 589832 | tf_op jit(solution)/shard_map/ppermute | solution.py:391
  74.5 0.1 collective-permute-start.11
  74.6 12.1 %collective-permute-done.10.outer = f32[12,32,128]{2,1,0:T(8,128)S(1)} collective-permute-done((f32[12,32,128]{2,1,0:T(8,128)S(1)}, f32[12,32,128]{2,1,0:T(8,128)S(1)}, u32[]{:S(2)}, u32[]{:S(2)}) %collective-permute-start.10) | collective-permute-done | bytes 196640 | tf_op jit(solution)/shard_map/ppermute | solution.py:391
  86.7 0.0 collective-permute-done.11.inner
  86.7 1.1 %meridional.3 = f32[4,4,32,128]{3,2,1,0:T(8,128)} custom-call(f32[4,4,32,128]{3,2,1,0:T(8,128)S(1)} %get-tuple-element.37.block, f32[32,1,128]{2,1,0:T(1,128)S(1)} %all_to_all.5.wind, f32[12,32,128]{2,1,0:T(8,128)S(1)} %collective-permute-done.10.outer, f32[12,32,128]{2,1,0:T(8,128)S(1)} %collective-permute-done.11.inner, ...), custom_call_target="tpu_custom_call" | custom-call | tf_op jit(solution)/shard_map/meridional/pallas_call | solution.py:335
Async XLA Ops:
  8.9 33.6 %collective-permute-start = (f32[4,3,16,128]{3,2,1,0:T(8,128)S(1)}, f32[4,3,16,128]{3,2,1,0:T(8,128)S(1)}, u32[]{:S(2)}, u32[]{:S(2)}) collective-permute-start(f32[4,3,16,128]{3,2,1,0:T(8,128)S(1)} %get-tuple-element.25), channel_id=1, source_target_pairs={{0,1},{1,2},{2,3},{3,4},{4,5},{5,6},{6,7},{7,8},{8,9},{9,10},{10,1... | collective-permute-start | bytes 294920 | tf_op jit(solution)/shard_map/ppermute | solution.py:383
  9.0 33.5 %collective-permute-start.1 = (f32[4,3,16,128]{3,2,1,0:T(8,128)S(1)}, f32[4,3,16,128]{3,2,1,0:T(8,128)S(1)}, u32[]{:S(2)}, u32[]{:S(2)}) collective-permute-start(f32[4,3,16,128]{3,2,1,0:T(8,128)S(1)} %get-tuple-element.26), channel_id=1, source_target_pairs={{0,1},{1,2},{2,3},{3,4},{4,5},{5,6},{6,7},{7,8},{8,9},{9,10},{10,1... | collective-permute-start | bytes 294920 | tf_op jit(solution)/shard_map/ppermute | solution.py:383
  10.6 31.9 %collective-permute-start.2 = (f32[4,3,16,128]{3,2,1,0:T(8,128)S(1)}, f32[4,3,16,128]{3,2,1,0:T(8,128)S(1)}, u32[]{:S(2)}, u32[]{:S(2)}) collective-permute-start(f32[4,3,16,128]{3,2,1,0:T(8,128)S(1)} %get-tuple-element.27), channel_id=1, source_target_pairs={{1,0},{2,1},{3,2},{4,3},{5,4},{6,5},{7,6},{8,7},{9,8},{10,9},{11,1... | collective-permute-start | bytes 294920 | tf_op jit(solution)/shard_map/ppermute | solution.py:383
  12.9 29.6 %collective-permute-start.3 = (f32[4,3,16,128]{3,2,1,0:T(8,128)S(1)}, f32[4,3,16,128]{3,2,1,0:T(8,128)S(1)}, u32[]{:S(2)}, u32[]{:S(2)}) collective-permute-start(f32[4,3,16,128]{3,2,1,0:T(8,128)S(1)} %get-tuple-element.28), channel_id=1, source_target_pairs={{1,0},{2,1},{3,2},{4,3},{5,4},{6,5},{7,6},{8,7},{9,8},{10,9},{11,1... | collective-permute-start | bytes 294920 | tf_op jit(solution)/shard_map/ppermute | solution.py:383
  42.9 19.5 %collective-permute-start.4 = (f32[13,32,128]{2,1,0:T(8,128)S(1)}, f32[13,32,128]{2,1,0:T(8,128)S(1)}, u32[]{:S(2)}, u32[]{:S(2)}) collective-permute-start(f32[13,32,128]{2,1,0:T(8,128)S(1)} %get-tuple-element.30), channel_id=1, source_target_pairs={{0,0},{32,64},{64,32},{96,128},{128,96},{160,192},{192,160},{224,2... | collective-permute-start | bytes 638984 | tf_op jit(solution)/shard_map/ppermute | solution.py:391
  47.0 15.4 %collective-permute-start.5 = (f32[13,32,128]{2,1,0:T(8,128)S(1)}, f32[13,32,128]{2,1,0:T(8,128)S(1)}, u32[]{:S(2)}, u32[]{:S(2)}) collective-permute-start(f32[13,32,128]{2,1,0:T(8,128)S(1)} %get-tuple-element.31), channel_id=1, source_target_pairs={{0,32},{32,0},{64,96},{96,64},{128,160},{160,128},{192,224},{224,1... | collective-permute-start | bytes 638984 | tf_op jit(solution)/shard_map/ppermute | solution.py:390
  62.8 6.2 %collective-permute-start.6 = (f32[4,3,16,128]{3,2,1,0:T(8,128)S(1)}, f32[4,3,16,128]{3,2,1,0:T(8,128)S(1)}, u32[]{:S(2)}, u32[]{:S(2)}) collective-permute-start(f32[4,3,16,128]{3,2,1,0:T(8,128)S(1)} %get-tuple-element.33), channel_id=1, source_target_pairs={{0,1},{1,2},{2,3},{3,4},{4,5},{5,6},{6,7},{7,8},{8,9},{9,10},{10,1... | collective-permute-start | bytes 294920 | tf_op jit(solution)/shard_map/ppermute | solution.py:383
  62.9 7.2 %collective-permute-start.7 = (f32[4,3,16,128]{3,2,1,0:T(8,128)S(1)}, f32[4,3,16,128]{3,2,1,0:T(8,128)S(1)}, u32[]{:S(2)}, u32[]{:S(2)}) collective-permute-start(f32[4,3,16,128]{3,2,1,0:T(8,128)S(1)} %get-tuple-element.34), channel_id=1, source_target_pairs={{0,1},{1,2},{2,3},{3,4},{4,5},{5,6},{6,7},{7,8},{8,9},{9,10},{10,1... | collective-permute-start | bytes 294920 | tf_op jit(solution)/shard_map/ppermute | solution.py:383
  63.6 6.5 %collective-permute-start.8 = (f32[4,3,16,128]{3,2,1,0:T(8,128)S(1)}, f32[4,3,16,128]{3,2,1,0:T(8,128)S(1)}, u32[]{:S(2)}, u32[]{:S(2)}) collective-permute-start(f32[4,3,16,128]{3,2,1,0:T(8,128)S(1)} %get-tuple-element.35), channel_id=1, source_target_pairs={{1,0},{2,1},{3,2},{4,3},{5,4},{6,5},{7,6},{8,7},{9,8},{10,9},{11,1... | collective-permute-start | bytes 294920 | tf_op jit(solution)/shard_map/ppermute | solution.py:383
  66.8 5.3 %collective-permute-start.9 = (f32[4,3,16,128]{3,2,1,0:T(8,128)S(1)}, f32[4,3,16,128]{3,2,1,0:T(8,128)S(1)}, u32[]{:S(2)}, u32[]{:S(2)}) collective-permute-start(f32[4,3,16,128]{3,2,1,0:T(8,128)S(1)} %get-tuple-element.36), channel_id=1, source_target_pairs={{1,0},{2,1},{3,2},{4,3},{5,4},{6,5},{7,6},{8,7},{9,8},{10,9},{11,1... | collective-permute-start | bytes 294920 | tf_op jit(solution)/shard_map/ppermute | solution.py:383
  72.5 14.2 %collective-permute-start.10 = (f32[12,32,128]{2,1,0:T(8,128)S(1)}, f32[12,32,128]{2,1,0:T(8,128)S(1)}, u32[]{:S(2)}, u32[]{:S(2)}) collective-permute-start(f32[12,32,128]{2,1,0:T(8,128)S(1)} %get-tuple-element.38), channel_id=1, source_target_pairs={{0,0},{32,64},{64,32},{96,128},{128,96},{160,192},{192,160},{224,2... | collective-permute-start | bytes 589832 | tf_op jit(solution)/shard_map/ppermute | solution.py:391
  74.5 12.2 %collective-permute-start.11 = (f32[12,32,128]{2,1,0:T(8,128)S(1)}, f32[12,32,128]{2,1,0:T(8,128)S(1)}, u32[]{:S(2)}, u32[]{:S(2)}) collective-permute-start(f32[12,32,128]{2,1,0:T(8,128)S(1)} %get-tuple-element.39), channel_id=1, source_target_pairs={{0,32},{32,0},{64,96},{96,64},{128,160},{160,128},{192,224},{224,1... | collective-permute-start | bytes 589832 | tf_op jit(solution)/shard_map/ppermute | solution.py:390
